TPU v7x, 32 devices: a whole 2x2x4 slice. The times are simulated.
32 devices in a mesh: groups: 2 (over x), vocab: 8 (over z, y), tok: 2 (over core).
Axes of the slice: x: 2, y: 2, z: 4, core: 2. Of those that a mesh axis runs over, the one named last changes fastest.
Arguments:
- teacher_hidden: bfloat16 [1024, 8192], P(('groups', 'tok'), 'vocab'), parts along dimension 0
- teacher_weight: bfloat16 [8192, 76032], P(None, ('vocab', 'tok')), may hold values from -0.1875 to 0.1875
- student_hidden: bfloat16 [1024, 2048], P(('groups', 'tok'), 'vocab'), parts along dimension 0
- student_weight: bfloat16 [2048, 76032], P(None, ('vocab', 'tok')), may hold values from -0.375 to 0.375
- loss_mask: int32 [1024], P(('groups', 'tok')), parts along dimension 0, may hold values 0 or 1
Outputs:
- kl_token: float32 [1024], P(('groups', 'tok')), parts along dimension 0
- grad_hidden: bfloat16 [1024, 2048], P(('groups', 'tok'), 'vocab'), parts along dimension 0
There are 2 independent parts, one for each index of `groups`. A program takes and returns all parts, laid end to end along the dimension named above; an argument that names none is the same for every part. Nothing has to cross between parts.
All inputs are finite; a program needn't handle non-finite values. No bound on the sum of `loss_mask` on one device may be relied on, other than what follows from the above.
Results may differ from a plain program's by a relative error of at most 0.0049.
Values may be sent and summed in bfloat16 or wider, within the bound.
No kernel may reach another device: no remote copies, remote signals or barrier semaphores. Data moves between devices by JAX's collectives and lax.ppermute only.
A program may use at most 576 MiB of HBM per device.

v0:
```python
import jax
import jax.numpy as jnp
from jax import lax
from jax.sharding import PartitionSpec as P

loss_scale = 16.0


def joined(part, axis, combine):
    gathered = jax.tree.map(lambda a: lax.all_gather(a, axis), part)

    def take(source):
        return jax.tree.map(lambda a: lax.dynamic_index_in_dim(a, source, 0, False), gathered)

    return lax.fori_loop(
        1, lax.axis_size(axis), lambda source, state: combine(state, take(source)), take(0)
    )


def contract(weight, block_part):
    return jnp.dot(block_part, weight, preferred_element_type=jnp.float32)


def merge_pair(earlier, later_one):
    peak_value = jnp.maximum(earlier[0], later_one[0])
    exp_total = earlier[1] * jnp.exp(earlier[0] - peak_value) + later_one[1] * jnp.exp(
        later_one[0] - peak_value
    )
    return (peak_value, exp_total)


def merge_triple(earlier, later_one):
    peak_value = jnp.maximum(earlier[0], later_one[0])
    exp_total = earlier[1] * jnp.exp(earlier[0] - peak_value) + later_one[1] * jnp.exp(
        later_one[0] - peak_value
    )
    return (peak_value, exp_total, earlier[2] + later_one[2])


def student_relaid(teacher_logp, student_hidden, student_weight, loss_mask):
    student_cols = lax.all_gather(student_weight, "tok", axis=1, tiled=True)
    student_logits = contract(
        student_cols, lax.all_gather(student_hidden, "vocab", axis=1, tiled=True)
    )
    teacher_prob = jnp.exp(teacher_logp)
    cross_term = jnp.sum(teacher_prob * (teacher_logp - student_logits), axis=1)
    student_peak = jnp.max(student_logits, axis=1)
    student_local = jnp.sum(jnp.exp(student_logits - student_peak[:, None]), axis=1)
    student_top, student_total, cross_sum = joined(
        (student_peak, student_local, cross_term), "vocab", merge_triple
    )
    student_lse = student_top + jnp.log(student_total)
    kl_token = cross_sum + student_lse
    student_prob = jnp.exp(student_logits - student_lse[:, None])
    mask_rows = loss_scale * loss_mask.astype(jnp.float32)
    grad_logits = (mask_rows[:, None] * (student_prob - teacher_prob)).astype(jnp.bfloat16)
    hidden_term = lax.dot_general(
        grad_logits, student_cols, (((1,), (1,)), ((), ())), preferred_element_type=jnp.float32
    )
    grad_share = lax.psum_scatter(hidden_term, "vocab", scatter_dimension=1, tiled=True)
    return (kl_token, grad_share.astype(jnp.bfloat16))


def shards(teacher_hidden, teacher_weight, student_hidden, student_weight, loss_mask):
    all_rows = lax.all_gather(teacher_hidden, "tok", axis=0, tiled=True)
    logits = contract(teacher_weight, lax.all_gather(all_rows, "vocab", axis=1, tiled=True))
    local_max = jnp.max(logits, axis=1)
    local_total = jnp.sum(jnp.exp(logits - local_max[:, None]), axis=1)
    peak_value, exp_total = joined((local_max, local_total), ("vocab", "tok"), merge_pair)
    log_probs = logits - (peak_value + jnp.log(exp_total))[:, None]
    teacher_logp = lax.all_to_all(log_probs, "tok", split_axis=0, concat_axis=1, tiled=True)
    return student_relaid(teacher_logp, student_hidden, student_weight, loss_mask)


def solution(mesh):
    return jax.shard_map(
        shards,
        mesh=mesh,
        in_specs=(
            P(("groups", "tok"), "vocab"),
            P(None, ("vocab", "tok")),
            P(("groups", "tok"), "vocab"),
            P(None, ("vocab", "tok")),
            P(("groups", "tok")),
        ),
        out_specs=(P(("groups", "tok")), P(("groups", "tok"), "vocab")),
        check_vma=False,
    )
```

profile of v0, /device:TPU:0, one launch (start us, length us, event | category | flops | bytes accessed | tf_op | source)
XLA Modules:
  0.0 443.1 jit_solution(13839526574209307998)
XLA Ops:
  7.2 0.7 all-gather.19.cloned.1.call-update
  7.9 13.4 %all-gather.19.cloned.1.call-done = bf16[512,1024]{1,0:T(8,128)(2,1)} async-done(((bf16[256,1024]{1,0:T(8,128)(2,1)}), bf16[512,1024]{1,0:T(8,128)(2,1)}) %all-gather.19.cloned.1.call-update) | async-done | bytes 1048592 | tf_op jit(solution)/shard_map/all_gather | solution.py:65
  21.4 0.7 all-gather.15.cloned.1.call-update
  22.8 126.9 %all-gather.21.cloned.1.call-done = bf16[512,8192]{1,0:T(8,128)(2,1)} async-done(((bf16[512,1024]{1,0:T(8,128)(2,1)}), bf16[512,8192]{1,0:T(8,128)(2,1)}) %all-gather.21.cloned.1.call-update) | async-done | bytes 8388624 | tf_op jit(solution)/shard_map/all_gather | solution.py:66
  149.6 48.4 %fusion.4 = (f32[512]{0:T(512)S(1)}, f32[512,4752]{0,1:T(8,128)S(1)}) fusion(bf16[512,8192]{1,0:T(8,128)(2,1)} %all-gather.21.cloned.1.call-done, bf16[8192,4752]{0,1:T(8,128)(2,1)} %param.10), kind=kOutput, calls=%fused_computation.26 | convolution fusion | flops 39865098240 | bytes 95979520 | tf_op jit(solution)/shard_map/dot_general | solution.py:21
  198.0 7.3 %copy-done = f32[512,4752]{0,1:T(8,128)} copy-done((f32[512,4752]{0,1:T(8,128)}, f32[512,4752]{0,1:T(8,128)S(1)}, u32[]{:S(2)}) %copy-start) | copy-done | bytes 9732120
  205.3 1.3 exponential_reduce_fusion
  206.7 17.7 %all-gather.8 = f32[16,1,512]{2,1,0:T(1,128)S(1)} all-gather(f32[1,1,512]{2,1,0:T(1,128)S(1)} %bitcast.81), channel_id=5, replica_groups=mesh['groups'=2,'vocab'=8,'tok'=2] {'vocab','tok'}, dimensions={0}, use_global_device_ids=true | all-gather | bytes 34816 | tf_op jit(solution)/shard_map/all_gather | solution.py:10
  224.3 18.7 %all-gather.7 = f32[16,1,512]{2,1,0:T(1,128)S(1)} all-gather(f32[1,1,512]{2,1,0:T(1,128)S(1)} %bitcast.80), channel_id=4, replica_groups=mesh['groups'=2,'vocab'=8,'tok'=2] {'vocab','tok'}, dimensions={0}, use_global_device_ids=true | all-gather | bytes 34816 | tf_op jit(solution)/shard_map/all_gather | solution.py:10
  243.0 0.9 while.36
  243.9 5.0 %broadcast_subtract_fusion = f32[512,4752]{0,1:T(8,128)S(1)} fusion(f32[512,4752]{0,1:T(8,128)} %copy-done, f32[512]{0:T(512)S(1)} %log_add_fusion), kind=kLoop, calls=%fused_computation.15 | loop fusion | flops 2433024 | bytes 19466240 | tf_op jit(solution)/shard_map/sub | solution.py:70
  248.9 4.2 copy.21
  253.1 7.4 %all-to-all-start = ((f32[2,256,4752]{1,2,0:T(8,128)}), f32[2,256,4752]{1,2,0:T(8,128)}, u32[]{:S(2)}, u32[]{:S(2)}) async-start(f32[2,256,4752]{1,2,0:T(8,128)} %bitcast.64), calls=%async_computation | async-start | bytes 19464192 | tf_op jit(solution)/shard_map/all_to_all | solution.py:71
  260.8 20.8 %fusion.3 = (f32[256]{0:T(256)S(1)}, f32[256,9504]{0,1:T(8,128)}) fusion(bf16[256,2048]{1,0:T(8,128)(2,1)} %all-gather.15.cloned.1.call-done, bf16[2048,9504]{0,1:T(8,128)(2,1)} %all-gather.17.cloned.1.call-done), kind=kOutput, calls=%fused_computation.25 | convolution fusion | flops 9968099328 | bytes 49710080 | tf_op jit(solution)/shard_map/dot_general | solution.py:21
  281.7 7.9 %fusion.1 = (f32[256]{0:T(256)S(1)}, f32[256]{0:T(256)S(1)}) fusion(f32[256,9504]{0,1:T(8,128)} %get-tuple-element.355, f32[2,256,4752]{1,2,0:T(8,128)} %all-to-all-done, f32[256]{0:T(256)S(1)} %get-tuple-element.354), kind=kLoop, calls=%fused_computation.11 | loop fusion | flops 12164608 | bytes 19467264 | tf_op jit(solution)/shard_map/reduce_sum | solution.py:46
  289.6 16.8 %all-gather.6 = f32[8,1,256]{2,1,0:T(1,128)S(1)} all-gather(f32[1,1,256]{2,1,0:T(1,128)S(1)} %bitcast.84), channel_id=3, replica_groups=mesh['groups'=2,'vocab'=8,'tok'=2] {'vocab'}, dimensions={0}, use_global_device_ids=true | all-gather | bytes 9216 | tf_op jit(solution)/shard_map/all_gather | solution.py:10
  306.4 17.8 %all-gather.9 = f32[8,1,256]{2,1,0:T(1,128)S(1)} all-gather(f32[1,1,256]{2,1,0:T(1,128)S(1)} %bitcast.83), channel_id=6, replica_groups=mesh['groups'=2,'vocab'=8,'tok'=2] {'vocab'}, dimensions={0}, use_global_device_ids=true | all-gather | bytes 9216 | tf_op jit(solution)/shard_map/all_gather | solution.py:10
  324.1 16.8 %all-gather.5 = f32[8,1,256]{2,1,0:T(1,128)S(1)} all-gather(f32[1,1,256]{2,1,0:T(1,128)S(1)} %bitcast.82), channel_id=2, replica_groups=mesh['groups'=2,'vocab'=8,'tok'=2] {'vocab'}, dimensions={0}, use_global_device_ids=true | all-gather | bytes 9216 | tf_op jit(solution)/shard_map/all_gather | solution.py:10
  340.9 0.6 while.37
  341.5 0.6 fusion.2
  342.1 7.9 %multiply_convert_fusion = bf16[256,9504]{0,1:T(8,128)(2,1)S(1)} fusion(f32[256,9504]{0,1:T(8,128)} %get-tuple-element.355, f32[2,256,4752]{1,2,0:T(8,128)} %all-to-all-done, f32[256]{0:T(256)S(1)} %get-tuple-element.349, f32[256]{0:T(256)S(1)} %convert_multiply_fusion), kind=kLoop, calls=%fused_computation.12 | loop fusion | flops 9732096 | bytes 24332288 | tf_op jit(solution)/shard_map/convert_element_type | solution.py:56
  350.0 18.2 %fusion.5 = f32[256,2048]{1,0:T(8,128)} fusion(bf16[256,9504]{0,1:T(8,128)(2,1)S(1)} %multiply_convert_fusion, bf16[2048,9504]{0,1:T(8,128)(2,1)} %all-gather.17.cloned.1.call-done), kind=kOutput, calls=%fused_computation.27 | convolution fusion | flops 9965666304 | bytes 45891584 | tf_op jit(solution)/shard_map/dot_general | solution.py:57
  368.2 66.7 %reduce-scatter.2.cloned.1.call-done = f32[256,256]{1,0:T(8,128)} async-done(((f32[256,2048]{1,0:T(8,128)}), f32[256,256]{1,0:T(8,128)}) %reduce-scatter.2.cloned.1.call-update) | async-done | bytes 262160 | tf_op jit(solution)/shard_map/reduce_scatter | solution.py:60
  434.9 1.6 convert_element_type.11
  (84 shorter events, 1.9 us)
Async XLA Ops:
  7.2 14.1 %all-gather.19.cloned.1.call-start = ((), (), s32[]{:S(2)}) async-start(), calls=%async_computation.4 | async-start | bytes 1572864 | tf_op jit(solution)/shard_map/all_gather | solution.py:65
  7.9 141.7 %all-gather.21.cloned.1.call-start = ((), (), s32[]{:S(2)}) async-start(), calls=%async_computation.5 | async-start | bytes 9437184 | tf_op jit(solution)/shard_map/all_gather | solution.py:66
  21.3 239.5 %all-gather.15.cloned.1.call-start = ((), (), s32[]{:S(2)}) async-start(), calls=%async_computation.2 | async-start | bytes 1179648 | tf_op jit(solution)/shard_map/all_gather | solution.py:43
  22.1 0.7 copy-start.1
  22.1 238.8 %all-gather.17.cloned.1.call-start = ((), (), s32[]{:S(2)}) async-start(), calls=%async_computation.3 | async-start | bytes 58392576 | tf_op jit(solution)/shard_map/all_gather | solution.py:41
  198.0 7.3 %copy-start = (f32[512,4752]{0,1:T(8,128)}, f32[512,4752]{0,1:T(8,128)S(1)}, u32[]{:S(2)}) copy-start(f32[512,4752]{0,1:T(8,128)S(1)} %get-tuple-element.357) | copy-start | bytes 29196292
  253.1 28.6 %all-to-all-start = ((f32[2,256,4752]{1,2,0:T(8,128)}), f32[2,256,4752]{1,2,0:T(8,128)}, u32[]{:S(2)}, u32[]{:S(2)}) async-start(f32[2,256,4752]{1,2,0:T(8,128)} %bitcast.64), calls=%async_computation | async-start | bytes 19464192 | tf_op jit(solution)/shard_map/all_to_all | solution.py:71
  260.6 174.4 %reduce-scatter.2.cloned.1.call-start = ((), (), s32[]{:S(2)}) async-start(), calls=%async_computation.6 | async-start | bytes 2359296 | tf_op jit(solution)/shard_map/reduce_scatter | solution.py:60
Sparse Core Ops, SparseCore 0:
  9.5 11.7 all-gather.18
  23.5 126.0 all-gather.20
  151.7 37.7 all-gather.14
  190.8 57.8 all-gather.16
  368.3 66.5 reduce-scatter.1
where the time goes:
time: 443 us
  waiting for transfers between devices  209 us (47%)
  blocking collectives  87.6 us (20%)
  matrix products  87.4 us (20%)
  other arithmetic  24.9 us (6%)
  between operations  13.9 us (3%)
  local copies, waits for them, and re-layouts  12 us (3%)
  starting transfers between devices  7.79 us (2%)
    all_gather x1, waiting for transfers between devices, shards(): lax.all_gather(all_rows, 'vocab', axis=1, tiled=True)  127 us
    all_gather x5, blocking collectives, joined(): gathered = jax.tree.map(lambda a: lax.all_gather(a, axis), part)  87.6 us
    dot_general x2, matrix products, contract(): return jnp.dot(block_part, weight, preferred_element_type=jnp.float32)  69.3 us
    reduce_scatter x1, waiting for transfers between devices, student_relaid(): lax.psum_scatter(hidden_term, 'vocab', scatter_dimension=1, tiled=True)  66.7 us
    dot_general x1, matrix products, student_relaid(): lax.dot_general(grad_logits, student_cols, (((1,), (1,)), ((), ())), pref...  18.2 us
    all_gather x1, waiting for transfers between devices, shards(): all_rows = lax.all_gather(teacher_hidden, 'tok', axis=0, tiled=True)  13.4 us
  transfers between devices with their start and end apart: 6, of which 3 were waited for; matrix products, arithmetic and copies ran while one was open for 18% of the time, Pallas kernels for 0%

commit v1 on v0

v1 whole, which is shorter than its diff:
```python
import functools

import jax
import jax.numpy as jnp
from jax import lax
from jax.experimental import pallas as pl
from jax.experimental.pallas import tpu as pltpu
from jax.sharding import PartitionSpec as P

loss_scale = 16.0
f32 = jnp.float32
bf16 = jnp.bfloat16
MIB = 1 << 20
NT = (((1,), (1,)), ((), ()))
TN = (((0,), (0,)), ((), ()))
WHOLE = pl.BlockSpec(memory_space=pltpu.VMEM)
SWAP = ((0, 1), (1, 0))


def rows_per_block(rows, cap):
    for count in range(1, rows // 16 + 1):
        if rows % (16 * count) == 0 and rows // count <= cap:
            return rows // count
    return rows


def pinned(array):
    return pltpu.with_memory_space_constraint(array, pltpu.VMEM)


def stage_kernel(picks, pieces, dt, first, last, block, off_ref, *refs):
    refs = list(refs)
    shards = len(picks)

    def take(count):
        taken = refs[:count]
        del refs[:count]
        return taken

    parts = take(shards * pieces)
    wt, ws = take(shards), take(shards)
    held = None if first else take(2)
    t_out, s_out = take(2)
    stats = take(1)[0] if last else None
    xt, xs = take(2)
    run = take(1)[0] if last else None
    step = pl.program_id(0)

    @pl.when(step == 0)
    def _():
        for shard in range(shards):
            at = 0
            for part in parts[shard * pieces : (shard + 1) * pieces]:
                span = pl.ds(at, part.shape[0])
                xt[shard, span, :] = part[:, :dt]
                xs[shard, span, :] = part[:, dt:]
                at += part.shape[0]
        if last:
            run[...] = jnp.zeros_like(run)
            run[0:1, :] = jnp.full((1, run.shape[1]), -jnp.inf, f32)
            run[3:4, :] = jnp.full((1, run.shape[1]), -jnp.inf, f32)

    here = pl.ds(pl.multiple_of(step * block, 16), block)
    t = s = None
    for shard in range(shards):
        t_add = lax.dot_general(wt[shard][...], xt[shard], NT, preferred_element_type=f32)
        s_add = lax.dot_general(ws[shard][...], xs[shard], NT, preferred_element_type=f32)
        t = t_add if t is None else t + t_add
        s = s_add if s is None else s + s_add
    if not first:
        t = t + held[0][here, :]
        s = s + held[1][here, :]
    t_out[here, :] = t
    s_out[here, :] = s
    if last:
        t_top = jnp.maximum(run[0:1, :], jnp.max(t, axis=0, keepdims=True))
        s_top = jnp.maximum(run[3:4, :], jnp.max(s, axis=0, keepdims=True))
        t_exp = jnp.exp(t - t_top)
        t_fade = jnp.exp(run[0:1, :] - t_top)
        s_fade = jnp.exp(run[3:4, :] - s_top)
        run[1:2, :] = run[1:2, :] * t_fade + jnp.sum(t_exp, axis=0, keepdims=True)
        run[2:3, :] = run[2:3, :] * t_fade + jnp.sum(t_exp * (t - s), axis=0, keepdims=True)
        run[4:5, :] = run[4:5, :] * s_fade + jnp.sum(jnp.exp(s - s_top), axis=0, keepdims=True)
        run[0:1, :] = t_top
        run[3:4, :] = s_top

        @pl.when(step == pl.num_programs(0) - 1)
        def _():
            stats[...] = run[...]


def stage(shards, picks, offs, wt, ws, held, dt, ds, last):
    count, pieces = len(shards), len(shards[0])
    vocab = wt.shape[0]
    rows = sum(part.shape[0] for part in shards[0])
    block = rows_per_block(vocab, 800)
    parts = [part for shard in shards for part in shard]
    in_specs = [
        pl.BlockSpec(part.shape, lambda j, o: (0, 0), pipeline_mode=pl.Buffered(1))
        for part in parts
    ]
    for width in (dt, ds):
        in_specs += [
            pl.BlockSpec((block, width), lambda j, o, pick=pick: (j, o[pick])) for pick in picks
        ]
    args = parts + [wt] * count + [ws] * count
    aliases = {}
    if held is not None:
        aliases = {1 + len(args): 0, 2 + len(args): 1}
        in_specs += [WHOLE, WHOLE]
        args += [pinned(array) for array in held]
    logits = pltpu.VMEM((vocab, rows), f32)
    out_shape, out_specs = [logits, logits], [WHOLE, WHOLE]
    scratch = [pltpu.VMEM((count, rows, dt), bf16), pltpu.VMEM((count, rows, ds), bf16)]
    if last:
        out_shape.append(jax.ShapeDtypeStruct((8, rows), f32))
        out_specs.append(pl.BlockSpec((8, rows), lambda j, o: (0, 0)))
        scratch.append(pltpu.VMEM((8, rows), f32))
    return pl.pallas_call(
        functools.partial(stage_kernel, picks, pieces, dt, held is None, last, block),
        grid_spec=pltpu.PrefetchScalarGridSpec(
            num_scalar_prefetch=1,
            grid=(vocab // block,),
            in_specs=in_specs,
            out_specs=out_specs,
            scratch_shapes=scratch,
        ),
        out_shape=out_shape,
        input_output_aliases=aliases,
        compiler_params=pltpu.CompilerParams(vmem_limit_bytes=30 * MIB),
        cost_estimate=pl.CostEstimate(
            flops=2 * rows * count * (dt + ds) * vocab,
            bytes_accessed=2 * count * (dt + ds) * vocab,
            transcendentals=2 * rows * vocab if last else 0,
        ),
        name="stage_last" if last else "stage",
    )(offs, *args)


def grad_kernel(block, stats, t_ref, s_ref, ws, kl, own, other, total, lse):
    step = pl.program_id(0)
    rows = t_ref.shape[1]
    half = rows // 2

    @pl.when(step == 0)
    def _():
        sides = []
        for source in range(stats.shape[0]):
            both = stats[source]
            sides.append(both[:8])
            sides.append(jnp.concatenate([both[8:, half:], both[8:, :half]], axis=1))
        t_top = functools.reduce(jnp.maximum, [side[0:1] for side in sides])
        s_top = functools.reduce(jnp.maximum, [side[3:4] for side in sides])
        t_sum = sum(side[1:2] * jnp.exp(side[0:1] - t_top) for side in sides)
        cross = sum(side[2:3] * jnp.exp(side[0:1] - t_top) for side in sides)
        s_sum = sum(side[4:5] * jnp.exp(side[3:4] - s_top) for side in sides)
        t_lse = t_top + jnp.log(t_sum)
        s_lse = s_top + jnp.log(s_sum)
        lse[0:1, :] = t_lse
        lse[1:2, :] = s_lse
        kl[...] = cross / t_sum - t_lse + s_lse
        total[...] = jnp.zeros_like(total)

    here = pl.ds(pl.multiple_of(step * block, 16), block)
    student = jnp.exp(s_ref[here, :] - lse[1:2, :])
    teacher = jnp.exp(t_ref[here, :] - lse[0:1, :])
    grad = (student - teacher).astype(bf16)
    total[...] += lax.dot_general(grad, ws[...], TN, preferred_element_type=f32)

    @pl.when(step == pl.num_programs(0) - 1)
    def _():
        width = own.shape[2]
        for dest in range(own.shape[0]):
            own[dest] = total[:half, dest * width : (dest + 1) * width]
            other[dest] = total[half:, dest * width : (dest + 1) * width].astype(bf16)


def grad_partial(stats, t, s, ws, count):
    vocab, rows = t.shape
    features = ws.shape[1]
    block = rows_per_block(vocab, 800)
    half, width = rows // 2, features // count
    return pl.pallas_call(
        functools.partial(grad_kernel, block),
        grid=(vocab // block,),
        in_specs=[
            pl.BlockSpec(stats.shape, lambda j: (0, 0, 0), pipeline_mode=pl.Buffered(1)),
            WHOLE,
            WHOLE,
            pl.BlockSpec((block, features), lambda j: (j, 0)),
        ],
        out_specs=[
            pl.BlockSpec((1, rows), lambda j: (0, 0)),
            pl.BlockSpec((count, half, width), lambda j: (0, 0, 0)),
            pl.BlockSpec((count, half, width), lambda j: (0, 0, 0)),
        ],
        out_shape=[
            jax.ShapeDtypeStruct((1, rows), f32),
            jax.ShapeDtypeStruct((count, half, width), f32),
            jax.ShapeDtypeStruct((count, half, width), bf16),
        ],
        scratch_shapes=[pltpu.VMEM((rows, features), f32), pltpu.VMEM((8, rows), f32)],
        compiler_params=pltpu.CompilerParams(vmem_limit_bytes=30 * MIB),
        cost_estimate=pl.CostEstimate(
            flops=2 * rows * features * vocab,
            bytes_accessed=2 * features * vocab,
            transcendentals=2 * rows * vocab,
        ),
        name="grad",
    )(stats, pinned(t), pinned(s), ws)


def ring_order(count):
    return list(range(0, count, 2)) + list(range(count - 1, 0, -2))


def ringed(teacher_hidden, teacher_weight, student_hidden, student_weight, loss_mask):
    count = lax.axis_size("vocab")
    dt, ds = teacher_hidden.shape[1], student_hidden.shape[1]
    order = ring_order(count)
    place = {device: at for at, device in enumerate(order)}
    table = [[order[(place[d] + k) % count] for k in range(count)] for d in range(count)]
    offs = lax.dynamic_index_in_dim(
        jnp.array(table, jnp.int32), lax.axis_index("vocab"), 0, False
    )
    up = [(order[i], order[(i + 1) % count]) for i in range(count)]
    down = [(b, a) for a, b in up]

    def sibling(array):
        return lax.ppermute(array, "tok", SWAP)

    mine = jnp.concatenate([teacher_hidden, student_hidden], axis=1)
    half = mine.shape[0] // 2
    wt, ws = teacher_weight.T, student_weight.T
    from_low = from_high = mine
    held = stage([(mine, sibling(mine))], (0,), offs, wt, ws, None, dt, ds, count == 1)
    for hop in range(1, count // 2 + 1):
        if hop < count // 2:
            from_low = lax.ppermute(from_low, "vocab", up)
            from_high = lax.ppermute(from_high, "vocab", down)
            shards = [
                (from_low, sibling(from_low)),
                (from_high, sibling(from_high)),
            ]
            picks = (count - hop, hop)
        else:
            from_low = lax.ppermute(from_low[:half], "vocab", up)
            from_high = lax.ppermute(from_high[half:], "vocab", down)
            shards = [(from_low, from_high, sibling(from_low), sibling(from_high))]
            picks = (hop,)
        held = stage(shards, picks, offs, wt, ws, held, dt, ds, hop == count // 2)
    t, s, stats = held
    both = jnp.concatenate([stats, sibling(stats)], axis=0)
    every = lax.all_to_all(
        jnp.broadcast_to(both[None], (count,) + both.shape), "vocab", 0, 0, tiled=True
    )
    kl, own, other = grad_partial(every, t, s, ws, count)
    rows = teacher_hidden.shape[0]
    partial = (own + sibling(other).astype(f32)).astype(bf16)
    shares = lax.all_to_all(partial, "vocab", 0, 0, tiled=True)
    mask = loss_scale * loss_mask.astype(f32)
    grad = mask[:, None] * jnp.sum(shares.astype(f32), axis=0)
    return (kl[0, :rows], grad.astype(bf16))


def gathered(teacher_hidden, teacher_weight, student_hidden, student_weight, loss_mask):
    axes = ("vocab", "tok")

    def every_row(hidden):
        own = lax.all_gather(hidden, "vocab", axis=1, tiled=True)
        return lax.all_gather(own, "tok", axis=0, tiled=True)

    t = jnp.dot(every_row(teacher_hidden), teacher_weight, preferred_element_type=f32)
    s = jnp.dot(every_row(student_hidden), student_weight, preferred_element_type=f32)

    def log_total(logits):
        top = lax.pmax(jnp.max(logits, axis=1), axes)
        return top + jnp.log(lax.psum(jnp.sum(jnp.exp(logits - top[:, None]), axis=1), axes))

    t_log = t - log_total(t)[:, None]
    s_log = s - log_total(s)[:, None]
    teacher = jnp.exp(t_log)
    kl = lax.psum(jnp.sum(teacher * (t_log - s_log), axis=1), axes)
    grad = (jnp.exp(s_log) - teacher).astype(bf16)
    part = lax.dot_general(grad, student_weight, NT, preferred_element_type=f32)
    part = lax.psum_scatter(part, "tok", scatter_dimension=0, tiled=True)
    part = lax.psum_scatter(part, "vocab", scatter_dimension=1, tiled=True)
    rows = teacher_hidden.shape[0]
    mask = loss_scale * loss_mask.astype(f32)
    kl = lax.dynamic_slice_in_dim(kl, lax.axis_index("tok") * rows, rows)
    return (kl, (mask[:, None] * part).astype(bf16))


def shards(teacher_hidden, teacher_weight, student_hidden, student_weight, loss_mask):
    count = lax.axis_size("vocab")
    lanes = teacher_hidden.shape[1] % 128 == 0 and student_hidden.shape[1] % 128 == 0
    rows = teacher_hidden.shape[0] % 32 == 0 and teacher_weight.shape[1] % 16 == 0
    fits = lanes and rows and count % 2 == 0 and lax.axis_size("tok") == 2
    run = ringed if fits else gathered
    return run(teacher_hidden, teacher_weight, student_hidden, student_weight, loss_mask)


def solution(mesh):
    return jax.shard_map(
        shards,
        mesh=mesh,
        in_specs=(
            P(("groups", "tok"), "vocab"),
            P(None, ("vocab", "tok")),
            P(("groups", "tok"), "vocab"),
            P(None, ("vocab", "tok")),
            P(("groups", "tok")),
        ),
        out_specs=(P(("groups", "tok")), P(("groups", "tok"), "vocab")),
        check_vma=False,
    )
```

time: 443 us -> 184 us (0.42)
  waiting for transfers between devices: 209 us -> 46.6 us
  Pallas kernels: 0 us -> 101 us
  matrix products: 87.4 us -> 0 us
  blocking collectives: 87.6 us -> 15.1 us
  other arithmetic: 24.9 us -> 2.21 us
  between operations: 13.9 us -> 0.77 us
  local copies, waits for them, and re-layouts: 12 us -> 3.32 us
  starting transfers between devices: 7.79 us -> 14.6 us
    all_gather x4 -> x0, waiting for transfers between devices: 140 us -> none  [the longest x1 127 us: shards(): lax.all_gather(all_rows, 'vocab', axis=1, tiled=True)]
    pallas_call x0 -> x6, Pallas kernels: none -> 101 us  [the longest x5 81.3 us: stage(): pl.pallas_call(functools.partial(stage_kernel, picks, pieces, dt, held is...]
    all_gather x5 -> x0, blocking collectives: 87.6 us -> none  [joined(): gathered = jax.tree.map(lambda a: lax.all_gather(a, axis), part)]
    dot_general x3 -> x0, matrix products: 87.4 us -> none  [the longest x2 69.3 us: contract(): return jnp.dot(block_part, weight, preferred_element_type=jnp.float32)]
    reduce_scatter x1 -> x0, waiting for transfers between devices: 66.7 us -> none  [student_relaid(): lax.psum_scatter(hidden_term, 'vocab', scatter_dimension=1, tiled=True)]
    all_to_all x1, waiting for transfers between devices: 0.01 us -> 25.7 us  [ringed(): shares = lax.all_to_all(partial, 'vocab', 0, 0, tiled=True)]
    ppermute x0 -> x19, waiting for transfers between devices: none -> 20.9 us  [the longest x3 17.1 us: ringed(): from_low = lax.ppermute(from_low, 'vocab', up)]
    all_to_all x0 -> x1, blocking collectives: none -> 15.1 us  [ringed(): lax.all_to_all(jnp.broadcast_to(both[None], (count,) + both.shape), 'voca...]
  transfers between devices with their start and end apart: 6 -> 20, of which waited for: 3 -> 5; matrix products, arithmetic and copies ran while one was open for 18% -> 1% of each run, Pallas kernels for 0% -> 36%
where the time goes in v1:
time: 184 us; the launch traced here: 183 us
  Pallas kernels  101 us (55%)
  waiting for transfers between devices  46.6 us (25%)
  blocking collectives  15.1 us (8%)
  starting transfers between devices  14.6 us (8%)
  local copies, waits for them, and re-layouts  3.32 us (2%)
  other arithmetic  2.21 us (1%)
    pallas_call x5, Pallas kernels, stage(): pl.pallas_call(functools.partial(stage_kernel, picks, pieces, dt, held is...  81.3 us
    all_to_all x1, waiting for transfers between devices, ringed(): shares = lax.all_to_all(partial, 'vocab', 0, 0, tiled=True)  25.7 us
    pallas_call x1, Pallas kernels, grad_partial(): pl.pallas_call(functools.partial(grad_kernel, block), grid=(vocab // bloc...  19.5 us
    ppermute x3, waiting for transfers between devices, ringed(): from_low = lax.ppermute(from_low, 'vocab', up)  17.1 us
    all_to_all x1, blocking collectives, ringed(): lax.all_to_all(jnp.broadcast_to(both[None], (count,) + both.shape), 'voca...  15.1 us
    ppermute x3, starting transfers between devices, ringed(): from_low = lax.ppermute(from_low, 'vocab', up)  6.67 us
    ppermute x11, waiting for transfers between devices, sibling(): return lax.ppermute(array, 'tok', SWAP)  3.77 us
  transfers between devices with their start and end apart: 20, of which 5 were waited for; matrix products, arithmetic and copies ran while one was open for 1% of the time, Pallas kernels for 36%

profile of v1, /device:TPU:0, one launch (start us, length us, event | category | flops | bytes accessed | tf_op | source)
XLA Modules:
  0.0 183.4 jit_solution(7620117888151129424)
XLA Ops:
  0.6 1.1 constant_dynamic-update-slice_fusion.1
  1.7 0.9 constant_dynamic-update-slice_fusion.refs_0_
  2.6 3.1 %collective-permute-start = (bf16[256,1280]{1,0:T(8,128)(2,1)S(1)}, bf16[256,1280]{1,0:T(8,128)(2,1)S(1)}, u32[]{:S(2)}, u32[]{:S(2)}) collective-permute-start(bf16[256,1280]{1,0:T(8,128)(2,1)S(1)} %constant_dynamic-update-slice_fusion.refs_0_), channel_id=1, source_target_pairs={{0,4},{4,8},{8,12},{12,14},{14,10},{10,6},{6,2},{2,0},{1,5},{5,9},... | collective-permute-start | bytes 1966088 | tf_op jit(solution)/shard_map/ppermute | solution.py:239
  5.7 14.7 %collective-permute-done.refs_0_ = bf16[256,1280]{1,0:T(8,128)(2,1)S(1)} collective-permute-done((bf16[256,1280]{1,0:T(8,128)(2,1)S(1)}, bf16[256,1280]{1,0:T(8,128)(2,1)S(1)}, u32[]{:S(2)}, u32[]{:S(2)}) %collective-permute-start) | collective-permute-done | bytes 655392 | tf_op jit(solution)/shard_map/ppermute | solution.py:239
  20.4 1.8 collective-permute-start.1
  22.6 0.7 dynamic-slice_bitcast_fusion.off_ref
  23.3 11.7 %stage.4 = (f32[4752,512]{1,0:T(8,128)S(1)}, f32[4752,512]{1,0:T(8,128)S(1)}) custom-call(s32[8]{0:T(128)S(1)} %dynamic-slice_bitcast_fusion.off_ref, bf16[256,1280]{1,0:T(8,128)(2,1)S(1)} %constant_dynamic-update-slice_fusion.refs_0_, bf16[256,1280]{1,0:T(8,128)(2,1)S(1)} %collective-permute-done.16.refs_1_, ...), custom_call_target="tpu_custom_call" | custom-call | flops 6228541440 | bytes 12165120 | tf_op jit(solution)/shard_map/stage/pallas_call | solution.py:119
  35.1 2.5 %collective-permute-done.1.refs_0_ = bf16[256,1280]{1,0:T(8,128)(2,1)S(1)} collective-permute-done((bf16[256,1280]{1,0:T(8,128)(2,1)S(1)}, bf16[256,1280]{1,0:T(8,128)(2,1)S(1)}, u32[]{:S(2)}, u32[]{:S(2)}) %collective-permute-start.1) | collective-permute-done | bytes 655392 | tf_op jit(solution)/shard_map/ppermute | solution.py:239
  37.5 1.8 collective-permute-start.2
  39.8 18.0 %stage.5 = (f32[4752,512]{1,0:T(8,128)S(1)}, f32[4752,512]{1,0:T(8,128)S(1)}) custom-call(s32[8]{0:T(128)S(1)} %dynamic-slice_bitcast_fusion.off_ref, bf16[256,1280]{1,0:T(8,128)(2,1)S(1)} %collective-permute-done.refs_0_, bf16[256,1280]{1,0:T(8,128)(2,1)S(1)} %collective-permute-done.14.refs_1_, ...), custom_call_target="tpu_custom_call", output_to_operand_aliasing={{0}: (9, {}), {1}: (10, {})} | custom-call | flops 12457082880 | bytes 24330240 | tf_op jit(solution)/shard_map/stage/pallas_call | solution.py:119
  57.9 1.8 %collective-permute-start.3 = (bf16[128,1280]{1,0:T(8,128)(2,1)S(1)}, bf16[128,1280]{1,0:T(8,128)(2,1)S(1)}, u32[]{:S(2)}, u32[]{:S(2)}) collective-permute-start(bf16[128,1280]{1,0:T(8,128)(2,1)S(1)} %slice.12), channel_id=1, source_target_pairs={{0,4},{4,8},{8,12},{12,14},{14,10},{10,6},{6,2},{2,0},{1,5},{5,9},... | collective-permute-start | bytes 983048 | tf_op jit(solution)/shard_map/ppermute | solution.py:247
  60.0 0.5 collective-permute-start.11
  60.5 18.0 %stage.6 = (f32[4752,512]{1,0:T(8,128)S(1)}, f32[4752,512]{1,0:T(8,128)S(1)}) custom-call(s32[8]{0:T(128)S(1)} %dynamic-slice_bitcast_fusion.off_ref, bf16[256,1280]{1,0:T(8,128)(2,1)S(1)} %collective-permute-done.1.refs_0_, bf16[256,1280]{1,0:T(8,128)(2,1)S(1)} %collective-permute-done.12.refs_1_, ...), custom_call_target="tpu_custom_call", output_to_operand_aliasing={{0}: (9, {}), {1}: (10, {})} | custom-call | flops 12457082880 | bytes 24330240 | tf_op jit(solution)/shard_map/stage/pallas_call | solution.py:119
  79.2 18.0 %stage.7 = (f32[4752,512]{1,0:T(8,128)S(1)}, f32[4752,512]{1,0:T(8,128)S(1)}) custom-call(s32[8]{0:T(128)S(1)} %dynamic-slice_bitcast_fusion.off_ref, bf16[256,1280]{1,0:T(8,128)(2,1)S(1)} %collective-permute-done.2.refs_0_, bf16[256,1280]{1,0:T(8,128)(2,1)S(1)} %collective-permute-done.10.refs_1_, ...), custom_call_target="tpu_custom_call", output_to_operand_aliasing={{0}: (9, {}), {1}: (10, {})} | custom-call | flops 12457082880 | bytes 24330240 | tf_op jit(solution)/shard_map/stage/pallas_call | solution.py:119
  97.2 15.6 %stage_last.1 = (f32[4752,512]{1,0:T(8,128)S(1)}, f32[4752,512]{1,0:T(8,128)S(1)}, f32[8,512]{1,0:T(8,128)S(1)}) custom-call(s32[8]{0:T(128)S(1)} %dynamic-slice_bitcast_fusion.off_ref, bf16[128,1280]{1,0:T(8,128)(2,1)S(1)} %collective-permute-done.3.refs_0_, ...), custom_call_target="tpu_custom_call", output_to_operand_aliasing={{0}: (7, {}), {1}: (8, {})} | custom-call | flops 6228541440 | bytes 12165120 | tf_op jit(solution)/shard_map/stage_last/pallas_call | solution.py:119
  112.9 1.1 collective-permute-done.17
  114.1 15.1 %all_to_all.10.stats = f32[8,16,512]{2,1,0:T(8,128)S(1)} all-to-all(f32[8,16,512]{2,1,0:T(8,128)S(1)} %broadcast_in_dim.2), channel_id=1, replica_groups=mesh['groups'=2,'vocab'=8,'tok'=2] {'vocab'}, dimensions={0} | all-to-all | bytes 524288 | tf_op jit(solution)/shard_map/all_to_all | solution.py:254
  129.2 19.5 %grad.1 = (f32[1,512]{1,0:T(1,128)S(1)}, f32[8,256,256]{2,1,0:T(8,128)S(1)}, bf16[8,256,256]{2,1,0:T(8,128)(2,1)S(1)}) custom-call(f32[8,16,512]{2,1,0:T(8,128)S(1)} %all_to_all.10.stats, f32[4752,512]{1,0:T(8,128)S(1)} %get-tuple-element.25.t_ref, f32[4752,512]{1,0:T(8,128)S(1)} %get-tuple-element.26.s_ref, bf16[4752,2048]{1,0:T(8,128)(2,1)} %bitcast.13), custom_call_target="tpu_custom_call" | custom-call | flops 9965666304 | bytes 19464192 | tf_op jit(solution)/shard_map/grad/pallas_call | solution.py:183
  148.7 2.6 %collective-permute-done.18 = bf16[8,256,256]{2,1,0:T(8,128)(2,1)S(1)} collective-permute-done((bf16[8,256,256]{2,1,0:T(8,128)(2,1)S(1)}, bf16[8,256,256]{2,1,0:T(8,128)(2,1)S(1)}, u32[]{:S(2)}, u32[]{:S(2)}) %collective-permute-start.18) | collective-permute-done | bytes 1048608 | tf_op jit(solution)/shard_map/ppermute | solution.py:230
  151.4 1.3 add_convert_fusion
  152.7 3.6 %all-to-all-start.1 = ((bf16[8,256,256]{2,1,0:T(8,128)(2,1)}), bf16[8,256,256]{2,1,0:T(8,128)(2,1)S(1)}, u32[]{:S(2)}, u32[]{:S(2)}) async-start(bf16[8,256,256]{2,1,0:T(8,128)(2,1)} %add_convert_fusion), calls=%async_computation.1 | async-start | bytes 2097152 | tf_op jit(solution)/shard_map/all_to_all | solution.py:260
  156.3 0.6 slice.11
  156.8 25.7 %all-to-all-done.1 = bf16[8,256,256]{2,1,0:T(8,128)(2,1)S(1)} async-done(((bf16[8,256,256]{2,1,0:T(8,128)(2,1)}), bf16[8,256,256]{2,1,0:T(8,128)(2,1)S(1)}, u32[]{:S(2)}, u32[]{:S(2)}) %all-to-all-start.1) | async-done | bytes 1048608 | tf_op jit(solution)/shard_map/all_to_all | solution.py:260
  182.6 0.8 multiply_convert_fusion
  (37 shorter events, 2.3 us)
Async XLA Ops:
  2.6 17.8 %collective-permute-start = (bf16[256,1280]{1,0:T(8,128)(2,1)S(1)}, bf16[256,1280]{1,0:T(8,128)(2,1)S(1)}, u32[]{:S(2)}, u32[]{:S(2)}) collective-permute-start(bf16[256,1280]{1,0:T(8,128)(2,1)S(1)} %constant_dynamic-update-slice_fusion.refs_0_), channel_id=1, source_target_pairs={{0,4},{4,8},{8,12},{12,14},{14,10},{10,6},{6,2},{2,0},{1,5},{5,9},... | collective-permute-start | bytes 1966088 | tf_op jit(solution)/shard_map/ppermute | solution.py:239
  5.7 16.5 %collective-permute-start.4 = (bf16[256,1280]{1,0:T(8,128)(2,1)S(1)}, bf16[256,1280]{1,0:T(8,128)(2,1)S(1)}, u32[]{:S(2)}, u32[]{:S(2)}) collective-permute-start(bf16[256,1280]{1,0:T(8,128)(2,1)S(1)} %constant_dynamic-update-slice_fusion.refs_0_), channel_id=1, source_target_pairs={{4,0},{8,4},{12,8},{14,12},{10,14},{6,10},{2,6},{0,2},{5,1},{9,5},... | collective-permute-start | bytes 1966088 | tf_op jit(solution)/shard_map/ppermute | solution.py:240
  5.7 17.6 %collective-permute-start.16 = (bf16[256,1280]{1,0:T(8,128)(2,1)S(1)}, bf16[256,1280]{1,0:T(8,128)(2,1)S(1)}, u32[]{:S(2)}, u32[]{:S(2)}) collective-permute-start(bf16[256,1280]{1,0:T(8,128)(2,1)S(1)} %constant_dynamic-update-slice_fusion.refs_0_), channel_id=1, source_target_pairs={{0,1},{1,0},{2,3},{3,2},{4,5},{5,4},{6,7},{7,6},{8,9},{9,8},{10,11... | collective-permute-start | bytes 1966088 | tf_op jit(solution)/shard_map/ppermute | solution.py:230
  20.4 19.2 %collective-permute-start.14 = (bf16[256,1280]{1,0:T(8,128)(2,1)S(1)}, bf16[256,1280]{1,0:T(8,128)(2,1)S(1)}, u32[]{:S(2)}, u32[]{:S(2)}) collective-permute-start(bf16[256,1280]{1,0:T(8,128)(2,1)S(1)} %collective-permute-done.refs_0_), channel_id=1, source_target_pairs={{0,1},{1,0},{2,3},{3,2},{4,5},{5,4},{6,7},{7,6},{8,9},{9,8},{10,11... | collective-permute-start | bytes 1966088 | tf_op jit(solution)/shard_map/ppermute | solution.py:230
  20.4 17.1 %collective-permute-start.1 = (bf16[256,1280]{1,0:T(8,128)(2,1)S(1)}, bf16[256,1280]{1,0:T(8,128)(2,1)S(1)}, u32[]{:S(2)}, u32[]{:S(2)}) collective-permute-start(bf16[256,1280]{1,0:T(8,128)(2,1)S(1)} %collective-permute-done.refs_0_), channel_id=1, source_target_pairs={{0,4},{4,8},{8,12},{12,14},{14,10},{10,6},{6,2},{2,0},{1,5},{5,9},... | collective-permute-start | bytes 1966088 | tf_op jit(solution)/shard_map/ppermute | solution.py:239
  22.2 17.6 %collective-permute-start.15 = (bf16[256,1280]{1,0:T(8,128)(2,1)S(1)}, bf16[256,1280]{1,0:T(8,128)(2,1)S(1)}, u32[]{:S(2)}, u32[]{:S(2)}) collective-permute-start(bf16[256,1280]{1,0:T(8,128)(2,1)S(1)} %collective-permute-done.4.refs_2_), channel_id=1, source_target_pairs={{0,1},{1,0},{2,3},{3,2},{4,5},{5,4},{6,7},{7,6},{8,9},{9,8},{10,11... | collective-permute-start | bytes 1966088 | tf_op jit(solution)/shard_map/ppermute | solution.py:230
  22.4 16.9 %collective-permute-start.5 = (bf16[256,1280]{1,0:T(8,128)(2,1)S(1)}, bf16[256,1280]{1,0:T(8,128)(2,1)S(1)}, u32[]{:S(2)}, u32[]{:S(2)}) collective-permute-start(bf16[256,1280]{1,0:T(8,128)(2,1)S(1)} %collective-permute-done.4.refs_2_), channel_id=1, source_target_pairs={{4,0},{8,4},{12,8},{14,12},{10,14},{6,10},{2,6},{0,2},{5,1},{9,5},... | collective-permute-start | bytes 1966088 | tf_op jit(solution)/shard_map/ppermute | solution.py:240
  37.5 22.5 %collective-permute-start.12 = (bf16[256,1280]{1,0:T(8,128)(2,1)S(1)}, bf16[256,1280]{1,0:T(8,128)(2,1)S(1)}, u32[]{:S(2)}, u32[]{:S(2)}) collective-permute-start(bf16[256,1280]{1,0:T(8,128)(2,1)S(1)} %collective-permute-done.1.refs_0_), channel_id=1, source_target_pairs={{0,1},{1,0},{2,3},{3,2},{4,5},{5,4},{6,7},{7,6},{8,9},{9,8},{10,11... | collective-permute-start | bytes 1966088 | tf_op jit(solution)/shard_map/ppermute | solution.py:230
  37.5 20.3 %collective-permute-start.2 = (bf16[256,1280]{1,0:T(8,128)(2,1)S(1)}, bf16[256,1280]{1,0:T(8,128)(2,1)S(1)}, u32[]{:S(2)}, u32[]{:S(2)}) collective-permute-start(bf16[256,1280]{1,0:T(8,128)(2,1)S(1)} %collective-permute-done.1.refs_0_), channel_id=1, source_target_pairs={{0,4},{4,8},{8,12},{12,14},{14,10},{10,6},{6,2},{2,0},{1,5},{5,9},... | collective-permute-start | bytes 1966088 | tf_op jit(solution)/shard_map/ppermute | solution.py:239
  39.3 21.2 %collective-permute-start.13 = (bf16[256,1280]{1,0:T(8,128)(2,1)S(1)}, bf16[256,1280]{1,0:T(8,128)(2,1)S(1)}, u32[]{:S(2)}, u32[]{:S(2)}) collective-permute-start(bf16[256,1280]{1,0:T(8,128)(2,1)S(1)} %collective-permute-done.5.refs_2_), channel_id=1, source_target_pairs={{0,1},{1,0},{2,3},{3,2},{4,5},{5,4},{6,7},{7,6},{8,9},{9,8},{10,11... | collective-permute-start | bytes 1966088 | tf_op jit(solution)/shard_map/ppermute | solution.py:230
  39.6 20.2 %collective-permute-start.6 = (bf16[256,1280]{1,0:T(8,128)(2,1)S(1)}, bf16[256,1280]{1,0:T(8,128)(2,1)S(1)}, u32[]{:S(2)}, u32[]{:S(2)}) collective-permute-start(bf16[256,1280]{1,0:T(8,128)(2,1)S(1)} %collective-permute-done.5.refs_2_), channel_id=1, source_target_pairs={{4,0},{8,4},{12,8},{14,12},{10,14},{6,10},{2,6},{0,2},{5,1},{9,5},... | collective-permute-start | bytes 1966088 | tf_op jit(solution)/shard_map/ppermute | solution.py:240
  57.9 20.7 %collective-permute-start.3 = (bf16[128,1280]{1,0:T(8,128)(2,1)S(1)}, bf16[128,1280]{1,0:T(8,128)(2,1)S(1)}, u32[]{:S(2)}, u32[]{:S(2)}) collective-permute-start(bf16[128,1280]{1,0:T(8,128)(2,1)S(1)} %slice.12), channel_id=1, source_target_pairs={{0,4},{4,8},{8,12},{12,14},{14,10},{10,6},{6,2},{2,0},{1,5},{5,9},... | collective-permute-start | bytes 983048 | tf_op jit(solution)/shard_map/ppermute | solution.py:247
  59.7 18.9 %collective-permute-start.7 = (bf16[128,1280]{1,0:T(8,128)(2,1)S(1)}, bf16[128,1280]{1,0:T(8,128)(2,1)S(1)}, u32[]{:S(2)}, u32[]{:S(2)}) collective-permute-start(bf16[128,1280]{1,0:T(8,128)(2,1)S(1)} %slice.13), channel_id=1, source_target_pairs={{4,0},{8,4},{12,8},{14,12},{10,14},{6,10},{2,6},{0,2},{5,1},{9,5},... | collective-permute-start | bytes 983048 | tf_op jit(solution)/shard_map/ppermute | solution.py:248
  60.0 19.1 %collective-permute-start.10 = (bf16[256,1280]{1,0:T(8,128)(2,1)S(1)}, bf16[256,1280]{1,0:T(8,128)(2,1)S(1)}, u32[]{:S(2)}, u32[]{:S(2)}) collective-permute-start(bf16[256,1280]{1,0:T(8,128)(2,1)S(1)} %collective-permute-done.2.refs_0_), channel_id=1, source_target_pairs={{0,1},{1,0},{2,3},{3,2},{4,5},{5,4},{6,7},{7,6},{8,9},{9,8},{10,11... | collective-permute-start | bytes 1966088 | tf_op jit(solution)/shard_map/ppermute | solution.py:230
  60.0 19.1 %collective-permute-start.11 = (bf16[256,1280]{1,0:T(8,128)(2,1)S(1)}, bf16[256,1280]{1,0:T(8,128)(2,1)S(1)}, u32[]{:S(2)}, u32[]{:S(2)}) collective-permute-start(bf16[256,1280]{1,0:T(8,128)(2,1)S(1)} %collective-permute-done.6.refs_2_), channel_id=1, source_target_pairs={{0,1},{1,0},{2,3},{3,2},{4,5},{5,4},{6,7},{7,6},{8,9},{9,8},{10,11... | collective-permute-start | bytes 1966088 | tf_op jit(solution)/shard_map/ppermute | solution.py:230
  78.6 18.6 %collective-permute-start.8 = (bf16[128,1280]{1,0:T(8,128)(2,1)S(1)}, bf16[128,1280]{1,0:T(8,128)(2,1)S(1)}, u32[]{:S(2)}, u32[]{:S(2)}) collective-permute-start(bf16[128,1280]{1,0:T(8,128)(2,1)S(1)} %collective-permute-done.3.refs_0_), channel_id=1, source_target_pairs={{0,1},{1,0},{2,3},{3,2},{4,5},{5,4},{6,7},{7,6},{8,9},{9,8},{10,11... | collective-permute-start | bytes 983048 | tf_op jit(solution)/shard_map/ppermute | solution.py:230
  78.7 18.5 %collective-permute-start.9 = (bf16[128,1280]{1,0:T(8,128)(2,1)S(1)}, bf16[128,1280]{1,0:T(8,128)(2,1)S(1)}, u32[]{:S(2)}, u32[]{:S(2)}) collective-permute-start(bf16[128,1280]{1,0:T(8,128)(2,1)S(1)} %collective-permute-done.7.refs_1_), channel_id=1, source_target_pairs={{0,1},{1,0},{2,3},{3,2},{4,5},{5,4},{6,7},{7,6},{8,9},{9,8},{10,11... | collective-permute-start | bytes 983048 | tf_op jit(solution)/shard_map/ppermute | solution.py:230
  112.8 1.2 collective-permute-start.17
  129.2 27.1 %copy-start = (s32[256]{0:T(256)S(1)}, s32[256]{0:T(256)}, u32[]{:S(2)}) copy-start(s32[256]{0:T(256)} %param.10) | copy-start | bytes 3076
  148.6 2.7 %collective-permute-start.18 = (bf16[8,256,256]{2,1,0:T(8,128)(2,1)S(1)}, bf16[8,256,256]{2,1,0:T(8,128)(2,1)S(1)}, u32[]{:S(2)}, u32[]{:S(2)}) collective-permute-start(bf16[8,256,256]{2,1,0:T(8,128)(2,1)S(1)} %get-tuple-element.29), channel_id=1, source_target_pairs={{0,1},{1,0},{2,3},{3,2},{4,5},{5,4},{6,7},{7,6},{8,9},{9,8},{10,11... | collective-permute-start | bytes 3145736 | tf_op jit(solution)/shard_map/ppermute | solution.py:230
  152.7 29.8 %all-to-all-start.1 = ((bf16[8,256,256]{2,1,0:T(8,128)(2,1)}), bf16[8,256,256]{2,1,0:T(8,128)(2,1)S(1)}, u32[]{:S(2)}, u32[]{:S(2)}) async-start(bf16[8,256,256]{2,1,0:T(8,128)(2,1)} %add_convert_fusion), calls=%async_computation.1 | async-start | bytes 2097152 | tf_op jit(solution)/shard_map/all_to_all | solution.py:260

commit v2 on v1

v2 whole, which is shorter than its diff:
```python
import functools

import jax
import jax.numpy as jnp
from jax import lax
from jax.experimental import pallas as pl
from jax.experimental.pallas import tpu as pltpu
from jax.sharding import PartitionSpec as P

loss_scale = 16.0
f32 = jnp.float32
bf16 = jnp.bfloat16
MIB = 1 << 20
last_block = 1024
NT = (((1,), (1,)), ((), ()))
TN = (((0,), (0,)), ((), ()))
WHOLE = pl.BlockSpec(memory_space=pltpu.VMEM)
SWAP = ((0, 1), (1, 0))


def rows_per_block(rows, cap):
    for count in range(1, rows // 8 + 1):
        if rows % (8 * count) == 0 and rows // count <= cap:
            return rows // count
    return rows


def pinned(array):
    return pltpu.with_memory_space_constraint(array, pltpu.VMEM)


def stage_kernel(count, pieces, dt, first, block, off_ref, *refs):
    refs = list(refs)

    def take(number):
        taken = refs[:number]
        del refs[:number]
        return taken

    parts = take(count * pieces)
    wt, ws = take(count), take(count)
    held = None if first else take(2)
    t_out, s_out = take(2)
    tops, stats = take(2) if len(refs) > 2 else (None, None)
    xt, xs = take(2)
    run = take(1)[0] if tops is not None else None
    step, steps = pl.program_id(0), pl.num_programs(0)
    vocab, rows = t_out.shape

    @pl.when(step == 0)
    def _():
        for shard in range(count):
            at = 0
            for part in parts[shard * pieces : (shard + 1) * pieces]:
                span = pl.ds(at, part.shape[0])
                xt[shard, span, :] = part[:, :dt]
                xs[shard, span, :] = part[:, dt:]
                at += part.shape[0]
        if run is not None:
            run[...] = jnp.zeros_like(run)
            run[0:1, :] = jnp.full((1, rows), -jnp.inf, f32)
            run[3:4, :] = jnp.full((1, rows), -jnp.inf, f32)

    def multiply(size):
        here = pl.ds(pl.multiple_of(step * block, 8), size)
        t = s = None
        for shard in range(count):
            t_add = lax.dot_general(wt[shard][:size], xt[shard], NT, preferred_element_type=f32)
            s_add = lax.dot_general(ws[shard][:size], xs[shard], NT, preferred_element_type=f32)
            t = t_add if t is None else t + t_add
            s = s_add if s is None else s + s_add
        if not first:
            t = t + held[0][here, :]
            s = s + held[1][here, :]
        if run is None:
            t_out[here, :] = t
            s_out[here, :] = s
            return
        t_top = jnp.max(t, axis=0, keepdims=True)
        s_top = jnp.max(s, axis=0, keepdims=True)
        t_exp = jnp.exp(t - t_top)
        s_exp = jnp.exp(s - s_top)
        t_out[here, :] = t_exp
        s_out[here, :] = s_exp
        tops[step, 0:1, :] = t_top
        tops[step, 1:2, :] = s_top
        t_new = jnp.maximum(run[0:1, :], t_top)
        s_new = jnp.maximum(run[3:4, :], s_top)
        t_old, t_add = jnp.exp(run[0:1, :] - t_new), jnp.exp(t_top - t_new)
        s_old, s_add = jnp.exp(run[3:4, :] - s_new), jnp.exp(s_top - s_new)
        t_sum = jnp.sum(t_exp, axis=0, keepdims=True)
        cross = jnp.sum(t_exp * (t - s), axis=0, keepdims=True)
        s_sum = jnp.sum(s_exp, axis=0, keepdims=True)
        run[1:2, :] = run[1:2, :] * t_old + t_sum * t_add
        run[2:3, :] = run[2:3, :] * t_old + cross * t_add
        run[4:5, :] = run[4:5, :] * s_old + s_sum * s_add
        run[0:1, :] = t_new
        run[3:4, :] = s_new

    by_block(step, vocab, block, multiply)
    if run is not None:

        @pl.when(step == steps - 1)
        def _():
            for dest in range(stats.shape[0]):
                stats[dest] = run[...]


def by_block(step, vocab, block, body):
    whole, tail = vocab // block, vocab % block
    if tail == 0:
        body(block)
        return
    if whole > 0:
        pl.when(step < whole)(functools.partial(body, block))
    pl.when(step == whole)(functools.partial(body, tail))


def stage(shards, picks, offs, wt, ws, held, dt, ds, copies=0):
    count, pieces = len(shards), len(shards[0])
    vocab = wt.shape[0]
    last = copies > 0
    rows = sum(part.shape[0] for part in shards[0])
    block = last_block if last else rows_per_block(vocab, 800)
    block = min(block, vocab)
    blocks = pl.cdiv(vocab, block)
    parts = [part for shard in shards for part in shard]
    in_specs = [
        pl.BlockSpec(part.shape, lambda j, o: (0, 0), pipeline_mode=pl.Buffered(1))
        for part in parts
    ]
    for width in (dt, ds):
        in_specs += [
            pl.BlockSpec((block, width), lambda j, o, pick=pick: (j, o[pick])) for pick in picks
        ]
    args = parts + [wt] * count + [ws] * count
    aliases = {}
    if held is not None:
        aliases = {1 + len(args): 0, 2 + len(args): 1}
        in_specs += [WHOLE, WHOLE]
        args += [pinned(array) for array in held]
    out_shape, out_specs = [pltpu.VMEM((vocab, rows), f32)] * 2, [WHOLE, WHOLE]
    scratch = [pltpu.VMEM((count, rows, dt), bf16), pltpu.VMEM((count, rows, ds), bf16)]
    if last:
        for shape in ((blocks, 8, rows), (copies, 8, rows)):
            out_shape.append(jax.ShapeDtypeStruct(shape, f32))
            out_specs.append(pl.BlockSpec(shape, lambda j, o: (0, 0, 0)))
        scratch.append(pltpu.VMEM((8, rows), f32))
    return pl.pallas_call(
        functools.partial(stage_kernel, count, pieces, dt, held is None, block),
        grid_spec=pltpu.PrefetchScalarGridSpec(
            num_scalar_prefetch=1,
            grid=(blocks,),
            in_specs=in_specs,
            out_specs=out_specs,
            scratch_shapes=scratch,
        ),
        out_shape=out_shape,
        input_output_aliases=aliases,
        compiler_params=pltpu.CompilerParams(vmem_limit_bytes=24 * MIB),
        cost_estimate=pl.CostEstimate(
            flops=2 * rows * count * (dt + ds) * vocab,
            bytes_accessed=2 * count * (dt + ds) * vocab,
            transcendentals=2 * rows * vocab if last else 0,
        ),
        name="stage_last" if last else "stage",
    )(offs, *args)


def grad_kernel(block, off_ref, stats, tops, t_exp, s_exp, ws, kl, own, other, total, lse):
    step = pl.program_id(0)
    vocab, rows = t_exp.shape
    half = rows // 2

    @pl.when(step == 0)
    def _():
        me = off_ref[off_ref.shape[0] - 1]
        sides = []
        for chip in range(stats.shape[0] // 2):
            sides.append(stats[2 * chip + me])
            mate = stats[2 * chip + 1 - me]
            sides.append(jnp.concatenate([mate[:, half:], mate[:, :half]], axis=1))
        t_top = functools.reduce(jnp.maximum, [side[0:1] for side in sides])
        s_top = functools.reduce(jnp.maximum, [side[3:4] for side in sides])
        t_sum = sum(side[1:2] * jnp.exp(side[0:1] - t_top) for side in sides)
        cross = sum(side[2:3] * jnp.exp(side[0:1] - t_top) for side in sides)
        s_sum = sum(side[4:5] * jnp.exp(side[3:4] - s_top) for side in sides)
        t_lse = t_top + jnp.log(t_sum)
        s_lse = s_top + jnp.log(s_sum)
        lse[0:1, :] = t_lse
        lse[1:2, :] = s_lse
        kl[...] = cross / t_sum - t_lse + s_lse
        total[...] = jnp.zeros_like(total)

    def add(size):
        here = pl.ds(pl.multiple_of(step * block, 8), size)
        t_scale = jnp.exp(tops[step, 0:1, :] - lse[0:1, :])
        s_scale = jnp.exp(tops[step, 1:2, :] - lse[1:2, :])
        grad = (s_exp[here, :] * s_scale - t_exp[here, :] * t_scale).astype(bf16)
        total[...] += lax.dot_general(grad, ws[:size], TN, preferred_element_type=f32)

    by_block(step, vocab, block, add)

    @pl.when(step == pl.num_programs(0) - 1)
    def _():
        width = own.shape[2]
        for dest in range(own.shape[0]):
            own[dest] = total[:half, dest * width : (dest + 1) * width]
            other[dest] = total[half:, dest * width : (dest + 1) * width].astype(bf16)


def grad_partial(offs, stats, tops, t_exp, s_exp, ws, count):
    vocab, rows = t_exp.shape
    features = ws.shape[1]
    block = min(last_block, vocab)
    shares = (count, rows // 2, features // count)

    def still(array):
        return pl.BlockSpec(
            array.shape, lambda j, o: (0, 0, 0), pipeline_mode=pl.Buffered(1)
        )

    return pl.pallas_call(
        functools.partial(grad_kernel, block),
        grid_spec=pltpu.PrefetchScalarGridSpec(
            num_scalar_prefetch=1,
            grid=(pl.cdiv(vocab, block),),
            in_specs=[
                still(stats),
                still(tops),
                WHOLE,
                WHOLE,
                pl.BlockSpec((block, features), lambda j, o: (j, 0)),
            ],
            out_specs=[
                pl.BlockSpec((1, rows), lambda j, o: (0, 0)),
                pl.BlockSpec(shares, lambda j, o: (0, 0, 0)),
                pl.BlockSpec(shares, lambda j, o: (0, 0, 0)),
            ],
            scratch_shapes=[pltpu.VMEM((rows, features), f32), pltpu.VMEM((8, rows), f32)],
        ),
        out_shape=[
            jax.ShapeDtypeStruct((1, rows), f32),
            jax.ShapeDtypeStruct(shares, f32),
            jax.ShapeDtypeStruct(shares, bf16),
        ],
        compiler_params=pltpu.CompilerParams(vmem_limit_bytes=24 * MIB),
        cost_estimate=pl.CostEstimate(
            flops=2 * rows * features * vocab,
            bytes_accessed=2 * features * vocab,
            transcendentals=0,
        ),
        name="grad",
    )(offs, stats, tops, pinned(t_exp), pinned(s_exp), ws)


def ring_order(count):
    return list(range(0, count, 2)) + list(range(count - 1, 0, -2))


def ringed(teacher_hidden, teacher_weight, student_hidden, student_weight, loss_mask):
    count = lax.axis_size("vocab")
    dt, ds = teacher_hidden.shape[1], student_hidden.shape[1]
    order = ring_order(count)
    place = {device: at for at, device in enumerate(order)}
    table = [[order[(place[d] + k) % count] for k in range(count)] for d in range(count)]
    offs = lax.dynamic_index_in_dim(
        jnp.array(table, jnp.int32), lax.axis_index("vocab"), 0, False
    )
    offs = jnp.concatenate([offs, lax.axis_index("tok").astype(jnp.int32)[None]])
    up = [(order[i], order[(i + 1) % count]) for i in range(count)]
    down = [(b, a) for a, b in up]

    def sibling(array):
        return lax.ppermute(array, "tok", SWAP)

    mine = jnp.concatenate([teacher_hidden, student_hidden], axis=1)
    half = mine.shape[0] // 2
    wt, ws = teacher_weight.T, student_weight.T
    from_low = from_high = mine
    run = functools.partial(stage, offs=offs, wt=wt, ws=ws, dt=dt, ds=ds)
    held, waiting, picks = None, [(mine, sibling(mine))], (0,)
    for hop in range(1, count // 2 + 1):
        final = hop == count // 2
        next_low = lax.ppermute(from_low[:half] if final else from_low, "vocab", up)
        next_high = lax.ppermute(from_high[half:] if final else from_high, "vocab", down)
        held = run(waiting, picks, held=held)
        from_low, from_high, *held = lax.optimization_barrier((next_low, next_high, *held))
        if final:
            waiting = [(from_low, from_high, sibling(from_low), sibling(from_high))]
            picks = (hop,)
        else:
            waiting = [(from_low, sibling(from_low)), (from_high, sibling(from_high))]
            picks = (count - hop, hop)
    t_exp, s_exp, tops, stats = run(waiting, picks, held=held, copies=2 * count)
    every = lax.all_to_all(stats, ("vocab", "tok"), 0, 0, tiled=True)
    kl, own, other = grad_partial(offs, every, tops, t_exp, s_exp, ws, count)
    rows = teacher_hidden.shape[0]
    partial = (own + sibling(other).astype(f32)).astype(bf16)
    shares = lax.all_to_all(partial, "vocab", 0, 0, tiled=True)
    mask = loss_scale * loss_mask.astype(f32)
    grad = mask[:, None] * jnp.sum(shares.astype(f32), axis=0)
    return (kl[0, :rows], grad.astype(bf16))


def gathered(teacher_hidden, teacher_weight, student_hidden, student_weight, loss_mask):
    axes = ("vocab", "tok")

    def every_row(hidden):
        own = lax.all_gather(hidden, "vocab", axis=1, tiled=True)
        return lax.all_gather(own, "tok", axis=0, tiled=True)

    t = jnp.dot(every_row(teacher_hidden), teacher_weight, preferred_element_type=f32)
    s = jnp.dot(every_row(student_hidden), student_weight, preferred_element_type=f32)

    def log_total(logits):
        top = lax.pmax(jnp.max(logits, axis=1), axes)
        return top + jnp.log(lax.psum(jnp.sum(jnp.exp(logits - top[:, None]), axis=1), axes))

    t_log = t - log_total(t)[:, None]
    s_log = s - log_total(s)[:, None]
    teacher = jnp.exp(t_log)
    kl = lax.psum(jnp.sum(teacher * (t_log - s_log), axis=1), axes)
    grad = (jnp.exp(s_log) - teacher).astype(bf16)
    part = lax.dot_general(grad, student_weight, NT, preferred_element_type=f32)
    part = lax.psum_scatter(part, "tok", scatter_dimension=0, tiled=True)
    part = lax.psum_scatter(part, "vocab", scatter_dimension=1, tiled=True)
    rows = teacher_hidden.shape[0]
    mask = loss_scale * loss_mask.astype(f32)
    kl = lax.dynamic_slice_in_dim(kl, lax.axis_index("tok") * rows, rows)
    return (kl, (mask[:, None] * part).astype(bf16))


def shards(teacher_hidden, teacher_weight, student_hidden, student_weight, loss_mask):
    count = lax.axis_size("vocab")
    lanes = teacher_hidden.shape[1] % 128 == 0 and student_hidden.shape[1] % 128 == 0
    rows = teacher_hidden.shape[0] % 32 == 0 and teacher_weight.shape[1] % 16 == 0
    fits = lanes and rows and count % 2 == 0 and count >= 4 and lax.axis_size("tok") == 2
    run = ringed if fits else gathered
    return run(teacher_hidden, teacher_weight, student_hidden, student_weight, loss_mask)


def solution(mesh):
    return jax.shard_map(
        shards,
        mesh=mesh,
        in_specs=(
            P(("groups", "tok"), "vocab"),
            P(None, ("vocab", "tok")),
            P(("groups", "tok"), "vocab"),
            P(None, ("vocab", "tok")),
            P(("groups", "tok")),
        ),
        out_specs=(P(("groups", "tok")), P(("groups", "tok"), "vocab")),
        check_vma=False,
    )
```

time: 184 us -> 168 us (0.913)
  waiting for transfers between devices: 46.6 us -> 37 us
  Pallas kernels: 101 us -> 94.1 us
    ppermute x8, waiting for transfers between devices: 17.1 us -> 5.67 us  [the longest x4 4.14 us: ringed(): next_low = lax.ppermute(from_low[:half] if final else from_low, 'vocab', up)]
    pallas_call x6, Pallas kernels: 101 us -> 94.1 us  [the longest x5 78.9 us: stage(): pl.pallas_call(functools.partial(stage_kernel, count, pieces, dt, held is...]
    ppermute x11 -> x10, waiting for transfers between devices: 3.77 us -> 5.62 us  [sibling(): return lax.ppermute(array, 'tok', SWAP)]
  transfers between devices with their start and end apart: 20 -> 19, of which waited for: 5 -> 9; matrix products, arithmetic and copies ran while one was open for 1% -> 1% of each run, Pallas kernels for 36% -> 38%
where the time goes in v2:
time: 168 us; the launch traced here: 167 us
  Pallas kernels  94.1 us (56%)
  waiting for transfers between devices  37 us (22%)
  starting transfers between devices  15.2 us (9%)
  blocking collectives  14.8 us (9%)
  local copies, waits for them, and re-layouts  3.3 us (2%)
  other arithmetic  2.29 us (1%)
    pallas_call x5, Pallas kernels, stage(): pl.pallas_call(functools.partial(stage_kernel, count, pieces, dt, held is...  78.9 us
    all_to_all x1, waiting for transfers between devices, ringed(): shares = lax.all_to_all(partial, 'vocab', 0, 0, tiled=True)  25.7 us
    pallas_call x1, Pallas kernels, grad_partial(): pl.pallas_call(functools.partial(grad_kernel, block), grid_spec=pltpu.Pre...  15.2 us
    all_to_all x1, blocking collectives, ringed(): every = lax.all_to_all(stats, ('vocab', 'tok'), 0, 0, tiled=True)  14.8 us
    ppermute x4, starting transfers between devices, ringed(): next_low = lax.ppermute(from_low[:half] if final else from_low, 'vocab', up)  7.5 us
    ppermute x10, waiting for transfers between devices, sibling(): return lax.ppermute(array, 'tok', SWAP)  5.62 us
    ppermute x4, waiting for transfers between devices, ringed(): next_low = lax.ppermute(from_low[:half] if final else from_low, 'vocab', up)  4.14 us
    all_to_all x1, starting transfers between devices, ringed(): shares = lax.all_to_all(partial, 'vocab', 0, 0, tiled=True)  3.56 us
  transfers between devices with their start and end apart: 19, of which 9 were waited for; matrix products, arithmetic and copies ran while one was open for 1% of the time, Pallas kernels for 38%

profile of v2, /device:TPU:0, one launch (start us, length us, event | category | flops | bytes accessed | tf_op | source)
XLA Modules:
  0.0 167.4 jit_solution(305175586204433298)
XLA Ops:
  0.6 1.1 constant_dynamic-update-slice_fusion.1
  1.7 0.9 constant_dynamic-update-slice_fusion.refs_0_
  2.6 0.5 collective-permute-start.2
  3.1 2.6 %collective-permute-start = (bf16[256,1280]{1,0:T(8,128)(2,1)S(1)}, bf16[256,1280]{1,0:T(8,128)(2,1)S(1)}, u32[]{:S(2)}, u32[]{:S(2)}) collective-permute-start(bf16[256,1280]{1,0:T(8,128)(2,1)S(1)} %constant_dynamic-update-slice_fusion.refs_0_), channel_id=1, source_target_pairs={{0,4},{4,8},{8,12},{12,14},{14,10},{10,6},{6,2},{2,0},{1,5},{5,9},... | collective-permute-start | bytes 1966088 | tf_op jit(solution)/shard_map/ppermute | solution.py:285
  5.8 0.7 dynamic-slice_bitcast_fusion
  6.6 10.3 %stage.4 = (f32[4752,512]{1,0:T(8,128)S(1)}, f32[4752,512]{1,0:T(8,128)S(1)}) custom-call(s32[9]{0:T(128)S(1)} %pad_add_fusion.off_ref, bf16[256,1280]{1,0:T(8,128)(2,1)S(1)} %constant_dynamic-update-slice_fusion.refs_0_, bf16[256,1280]{1,0:T(8,128)(2,1)S(1)} %collective-permute-done.2.refs_1_, bf16[4752,8192]{1,0:T(8,128)(2,1)} %bitcast.2.refs_2_.refs_4_.refs_5_, ...), custom_call_target="tpu_custom_call" | custom-call | flops 6228541440 | bytes 12165120 | tf_op jit(solution)/shard_map/stage/pallas_call | solution.py:149
  16.9 4.1 %collective-permute-done.refs_0_ = bf16[256,1280]{1,0:T(8,128)(2,1)S(1)} collective-permute-done((bf16[256,1280]{1,0:T(8,128)(2,1)S(1)}, bf16[256,1280]{1,0:T(8,128)(2,1)S(1)}, u32[]{:S(2)}, u32[]{:S(2)}) %collective-permute-start) | collective-permute-done | bytes 655392 | tf_op jit(solution)/shard_map/ppermute | solution.py:285
  21.1 1.5 collective-permute-done.1.refs_2_
  23.1 1.6 collective-permute-start.3
  25.6 17.9 %stage.5 = (f32[4752,512]{1,0:T(8,128)S(1)}, f32[4752,512]{1,0:T(8,128)S(1)}) custom-call(s32[9]{0:T(128)S(1)} %pad_add_fusion.off_ref, bf16[256,1280]{1,0:T(8,128)(2,1)S(1)} %collective-permute-done.refs_0_, bf16[256,1280]{1,0:T(8,128)(2,1)S(1)} %collective-permute-done.5.refs_1_, ...), custom_call_target="tpu_custom_call", output_to_operand_aliasing={{0}: (9, {}), {1}: (10, {})} | custom-call | flops 12457082880 | bytes 24330240 | tf_op jit(solution)/shard_map/stage/pallas_call | solution.py:149
  44.2 1.6 collective-permute-start.7
  46.7 17.9 %stage.6 = (f32[4752,512]{1,0:T(8,128)S(1)}, f32[4752,512]{1,0:T(8,128)S(1)}) custom-call(s32[9]{0:T(128)S(1)} %pad_add_fusion.off_ref, bf16[256,1280]{1,0:T(8,128)(2,1)S(1)} %collective-permute-done.3.refs_0_, bf16[256,1280]{1,0:T(8,128)(2,1)S(1)} %collective-permute-done.9.refs_1_, ...), custom_call_target="tpu_custom_call", output_to_operand_aliasing={{0}: (9, {}), {1}: (10, {})} | custom-call | flops 12457082880 | bytes 24330240 | tf_op jit(solution)/shard_map/stage/pallas_call | solution.py:149
  65.3 1.7 collective-permute-start.11
  67.8 17.9 %stage.7 = (f32[4752,512]{1,0:T(8,128)S(1)}, f32[4752,512]{1,0:T(8,128)S(1)}) custom-call(s32[9]{0:T(128)S(1)} %pad_add_fusion.off_ref, bf16[256,1280]{1,0:T(8,128)(2,1)S(1)} %collective-permute-done.7.refs_0_, bf16[256,1280]{1,0:T(8,128)(2,1)S(1)} %collective-permute-done.13.refs_1_, ...), custom_call_target="tpu_custom_call", output_to_operand_aliasing={{0}: (9, {}), {1}: (10, {})} | custom-call | flops 12457082880 | bytes 24330240 | tf_op jit(solution)/shard_map/stage/pallas_call | solution.py:149
  86.3 1.1 collective-permute-done.15.refs_2_
  87.9 14.7 %stage_last.1 = (f32[4752,512]{1,0:T(8,128)S(1)}, f32[4752,512]{1,0:T(8,128)S(1)}, f32[5,8,512]{2,1,0:T(8,128)S(1)}, f32[16,8,512]{2,1,0:T(8,128)S(1)}) custom-call(s32[9]{0:T(128)S(1)} %pad_add_fusion.off_ref, bf16[128,1280]{1,0:T(8,128)(2,1)S(1)} %collective-permute-done.11.refs_0_, ...), custom_call_target="tpu_custom_call", output_to_operand_aliasing={{0}: (7, {}), {1}: (8, {})} | custom-call | flops 6228541440 | bytes 12165120 | tf_op jit(solution)/shard_map/stage_last/pallas_call | solution.py:149
  102.6 14.8 %all_to_all.10.stats = f32[16,8,512]{2,1,0:T(8,128)S(1)} all-to-all(f32[16,8,512]{2,1,0:T(8,128)S(1)} %get-tuple-element.57), channel_id=1, replica_groups=mesh['groups'=2,'vocab'=8,'tok'=2] {'vocab','tok'}, dimensions={0} | all-to-all | bytes 524288 | tf_op jit(solution)/shard_map/all_to_all | solution.py:296
  117.5 15.2 %grad.1 = (f32[1,512]{1,0:T(1,128)S(1)}, f32[8,256,256]{2,1,0:T(8,128)S(1)}, bf16[8,256,256]{2,1,0:T(8,128)(2,1)S(1)}) custom-call(s32[9]{0:T(128)S(1)} %pad_add_fusion.off_ref, f32[16,8,512]{2,1,0:T(8,128)S(1)} %all_to_all.10.stats, f32[5,8,512]{2,1,0:T(8,128)S(1)} %get-tuple-element.58.tops, f32[4752,512]{1,0:T(8,128)S(1)} %get-tuple-element.59.t_exp, ...), custom_call_target="tpu_custom_call" | custom-call | flops 9965666304 | bytes 19464192 | tf_op jit(solution)/shard_map/grad/pallas_call | solution.py:223
  132.7 2.6 %collective-permute-done.17 = bf16[8,256,256]{2,1,0:T(8,128)(2,1)S(1)} collective-permute-done((bf16[8,256,256]{2,1,0:T(8,128)(2,1)S(1)}, bf16[8,256,256]{2,1,0:T(8,128)(2,1)S(1)}, u32[]{:S(2)}, u32[]{:S(2)}) %collective-permute-start.17) | collective-permute-done | bytes 1048608 | tf_op jit(solution)/shard_map/ppermute | solution.py:275
  135.4 1.3 add_convert_fusion
  136.7 3.6 %all-to-all-start.1 = ((bf16[8,256,256]{2,1,0:T(8,128)(2,1)}), bf16[8,256,256]{2,1,0:T(8,128)(2,1)S(1)}, u32[]{:S(2)}, u32[]{:S(2)}) async-start(bf16[8,256,256]{2,1,0:T(8,128)(2,1)} %add_convert_fusion), calls=%async_computation.1 | async-start | bytes 2097152 | tf_op jit(solution)/shard_map/all_to_all | solution.py:300
  140.3 0.6 slice.11
  140.8 25.7 %all-to-all-done.1 = bf16[8,256,256]{2,1,0:T(8,128)(2,1)S(1)} async-done(((bf16[8,256,256]{2,1,0:T(8,128)(2,1)}), bf16[8,256,256]{2,1,0:T(8,128)(2,1)S(1)}, u32[]{:S(2)}, u32[]{:S(2)}) %all-to-all-start.1) | async-done | bytes 1048608 | tf_op jit(solution)/shard_map/all_to_all | solution.py:300
  166.7 0.8 multiply_convert_fusion
  (34 shorter events, 5.7 us)
Async XLA Ops:
  2.6 4.0 %collective-permute-start.2 = (bf16[256,1280]{1,0:T(8,128)(2,1)S(1)}, bf16[256,1280]{1,0:T(8,128)(2,1)S(1)}, u32[]{:S(2)}, u32[]{:S(2)}) collective-permute-start(bf16[256,1280]{1,0:T(8,128)(2,1)S(1)} %constant_dynamic-update-slice_fusion.refs_0_), channel_id=1, source_target_pairs={{0,1},{1,0},{2,3},{3,2},{4,5},{5,4},{6,7},{7,6},{8,9},{9,8},{10,11... | collective-permute-start | bytes 1966088 | tf_op jit(solution)/shard_map/ppermute | solution.py:275
  3.1 17.9 %collective-permute-start = (bf16[256,1280]{1,0:T(8,128)(2,1)S(1)}, bf16[256,1280]{1,0:T(8,128)(2,1)S(1)}, u32[]{:S(2)}, u32[]{:S(2)}) collective-permute-start(bf16[256,1280]{1,0:T(8,128)(2,1)S(1)} %constant_dynamic-update-slice_fusion.refs_0_), channel_id=1, source_target_pairs={{0,4},{4,8},{8,12},{12,14},{14,10},{10,6},{6,2},{2,0},{1,5},{5,9},... | collective-permute-start | bytes 1966088 | tf_op jit(solution)/shard_map/ppermute | solution.py:285
  5.8 16.8 %collective-permute-start.1 = (bf16[256,1280]{1,0:T(8,128)(2,1)S(1)}, bf16[256,1280]{1,0:T(8,128)(2,1)S(1)}, u32[]{:S(2)}, u32[]{:S(2)}) collective-permute-start(bf16[256,1280]{1,0:T(8,128)(2,1)S(1)} %constant_dynamic-update-slice_fusion.refs_0_), channel_id=1, source_target_pairs={{4,0},{8,4},{12,8},{14,12},{10,14},{6,10},{2,6},{0,2},{5,1},{9,5},... | collective-permute-start | bytes 1966088 | tf_op jit(solution)/shard_map/ppermute | solution.py:286
  22.6 2.5 %collective-permute-start.5 = (bf16[256,1280]{1,0:T(8,128)(2,1)S(1)}, bf16[256,1280]{1,0:T(8,128)(2,1)S(1)}, u32[]{:S(2)}, u32[]{:S(2)}) collective-permute-start(bf16[256,1280]{1,0:T(8,128)(2,1)S(1)} %collective-permute-done.refs_0_), channel_id=1, source_target_pairs={{0,1},{1,0},{2,3},{3,2},{4,5},{5,4},{6,7},{7,6},{8,9},{9,8},{10,11... | collective-permute-start | bytes 1966088 | tf_op jit(solution)/shard_map/ppermute | solution.py:275
  22.6 3.0 %collective-permute-start.6 = (bf16[256,1280]{1,0:T(8,128)(2,1)S(1)}, bf16[256,1280]{1,0:T(8,128)(2,1)S(1)}, u32[]{:S(2)}, u32[]{:S(2)}) collective-permute-start(bf16[256,1280]{1,0:T(8,128)(2,1)S(1)} %collective-permute-done.1.refs_2_), channel_id=1, source_target_pairs={{0,1},{1,0},{2,3},{3,2},{4,5},{5,4},{6,7},{7,6},{8,9},{9,8},{10,11... | collective-permute-start | bytes 1966088 | tf_op jit(solution)/shard_map/ppermute | solution.py:275
  23.1 20.5 %collective-permute-start.3 = (bf16[256,1280]{1,0:T(8,128)(2,1)S(1)}, bf16[256,1280]{1,0:T(8,128)(2,1)S(1)}, u32[]{:S(2)}, u32[]{:S(2)}) collective-permute-start(bf16[256,1280]{1,0:T(8,128)(2,1)S(1)} %collective-permute-done.refs_0_), channel_id=1, source_target_pairs={{0,4},{4,8},{8,12},{12,14},{14,10},{10,6},{6,2},{2,0},{1,5},{5,9},... | collective-permute-start | bytes 1966088 | tf_op jit(solution)/shard_map/ppermute | solution.py:285
  24.7 18.9 %collective-permute-start.4 = (bf16[256,1280]{1,0:T(8,128)(2,1)S(1)}, bf16[256,1280]{1,0:T(8,128)(2,1)S(1)}, u32[]{:S(2)}, u32[]{:S(2)}) collective-permute-start(bf16[256,1280]{1,0:T(8,128)(2,1)S(1)} %collective-permute-done.1.refs_2_), channel_id=1, source_target_pairs={{4,0},{8,4},{12,8},{14,12},{10,14},{6,10},{2,6},{0,2},{5,1},{9,5},... | collective-permute-start | bytes 1966088 | tf_op jit(solution)/shard_map/ppermute | solution.py:286
  43.6 2.6 %collective-permute-start.10 = (bf16[256,1280]{1,0:T(8,128)(2,1)S(1)}, bf16[256,1280]{1,0:T(8,128)(2,1)S(1)}, u32[]{:S(2)}, u32[]{:S(2)}) collective-permute-start(bf16[256,1280]{1,0:T(8,128)(2,1)S(1)} %collective-permute-done.4.refs_2_), channel_id=1, source_target_pairs={{0,1},{1,0},{2,3},{3,2},{4,5},{5,4},{6,7},{7,6},{8,9},{9,8},{10,11... | collective-permute-start | bytes 1966088 | tf_op jit(solution)/shard_map/ppermute | solution.py:275
  43.8 2.9 %collective-permute-start.9 = (bf16[256,1280]{1,0:T(8,128)(2,1)S(1)}, bf16[256,1280]{1,0:T(8,128)(2,1)S(1)}, u32[]{:S(2)}, u32[]{:S(2)}) collective-permute-start(bf16[256,1280]{1,0:T(8,128)(2,1)S(1)} %collective-permute-done.3.refs_0_), channel_id=1, source_target_pairs={{0,1},{1,0},{2,3},{3,2},{4,5},{5,4},{6,7},{7,6},{8,9},{9,8},{10,11... | collective-permute-start | bytes 1966088 | tf_op jit(solution)/shard_map/ppermute | solution.py:275
  44.2 20.5 %collective-permute-start.7 = (bf16[256,1280]{1,0:T(8,128)(2,1)S(1)}, bf16[256,1280]{1,0:T(8,128)(2,1)S(1)}, u32[]{:S(2)}, u32[]{:S(2)}) collective-permute-start(bf16[256,1280]{1,0:T(8,128)(2,1)S(1)} %collective-permute-done.3.refs_0_), channel_id=1, source_target_pairs={{0,4},{4,8},{8,12},{12,14},{14,10},{10,6},{6,2},{2,0},{1,5},{5,9},... | collective-permute-start | bytes 1966088 | tf_op jit(solution)/shard_map/ppermute | solution.py:285
  45.8 18.9 %collective-permute-start.8 = (bf16[256,1280]{1,0:T(8,128)(2,1)S(1)}, bf16[256,1280]{1,0:T(8,128)(2,1)S(1)}, u32[]{:S(2)}, u32[]{:S(2)}) collective-permute-start(bf16[256,1280]{1,0:T(8,128)(2,1)S(1)} %collective-permute-done.4.refs_2_), channel_id=1, source_target_pairs={{4,0},{8,4},{12,8},{14,12},{10,14},{6,10},{2,6},{0,2},{5,1},{9,5},... | collective-permute-start | bytes 1966088 | tf_op jit(solution)/shard_map/ppermute | solution.py:286
  64.7 2.7 %collective-permute-start.13 = (bf16[256,1280]{1,0:T(8,128)(2,1)S(1)}, bf16[256,1280]{1,0:T(8,128)(2,1)S(1)}, u32[]{:S(2)}, u32[]{:S(2)}) collective-permute-start(bf16[256,1280]{1,0:T(8,128)(2,1)S(1)} %collective-permute-done.7.refs_0_), channel_id=1, source_target_pairs={{0,1},{1,0},{2,3},{3,2},{4,5},{5,4},{6,7},{7,6},{8,9},{9,8},{10,11... | collective-permute-start | bytes 1966088 | tf_op jit(solution)/shard_map/ppermute | solution.py:275
  64.9 2.9 %collective-permute-start.14 = (bf16[256,1280]{1,0:T(8,128)(2,1)S(1)}, bf16[256,1280]{1,0:T(8,128)(2,1)S(1)}, u32[]{:S(2)}, u32[]{:S(2)}) collective-permute-start(bf16[256,1280]{1,0:T(8,128)(2,1)S(1)} %collective-permute-done.8.refs_2_), channel_id=1, source_target_pairs={{0,1},{1,0},{2,3},{3,2},{4,5},{5,4},{6,7},{7,6},{8,9},{9,8},{10,11... | collective-permute-start | bytes 1966088 | tf_op jit(solution)/shard_map/ppermute | solution.py:275
  65.3 20.4 %collective-permute-start.11 = (bf16[128,1280]{1,0:T(8,128)(2,1)S(1)}, bf16[128,1280]{1,0:T(8,128)(2,1)S(1)}, u32[]{:S(2)}, u32[]{:S(2)}) collective-permute-start(bf16[128,1280]{1,0:T(8,128)(2,1)S(1)} %slice.9), channel_id=1, source_target_pairs={{0,4},{4,8},{8,12},{12,14},{14,10},{10,6},{6,2},{2,0},{1,5},{5,9},... | collective-permute-start | bytes 983048 | tf_op jit(solution)/shard_map/ppermute | solution.py:285
  67.0 18.8 %collective-permute-start.12 = (bf16[128,1280]{1,0:T(8,128)(2,1)S(1)}, bf16[128,1280]{1,0:T(8,128)(2,1)S(1)}, u32[]{:S(2)}, u32[]{:S(2)}) collective-permute-start(bf16[128,1280]{1,0:T(8,128)(2,1)S(1)} %slice.10), channel_id=1, source_target_pairs={{4,0},{8,4},{12,8},{14,12},{10,14},{6,10},{2,6},{0,2},{5,1},{9,5},... | collective-permute-start | bytes 983048 | tf_op jit(solution)/shard_map/ppermute | solution.py:286
  85.8 1.7 %collective-permute-start.15 = (bf16[128,1280]{1,0:T(8,128)(2,1)S(1)}, bf16[128,1280]{1,0:T(8,128)(2,1)S(1)}, u32[]{:S(2)}, u32[]{:S(2)}) collective-permute-start(bf16[128,1280]{1,0:T(8,128)(2,1)S(1)} %collective-permute-done.11.refs_0_), channel_id=1, source_target_pairs={{0,1},{1,0},{2,3},{3,2},{4,5},{5,4},{6,7},{7,6},{8,9},{9,8},{10,11... | collective-permute-start | bytes 983048 | tf_op jit(solution)/shard_map/ppermute | solution.py:275
  86.0 2.0 %collective-permute-start.16 = (bf16[128,1280]{1,0:T(8,128)(2,1)S(1)}, bf16[128,1280]{1,0:T(8,128)(2,1)S(1)}, u32[]{:S(2)}, u32[]{:S(2)}) collective-permute-start(bf16[128,1280]{1,0:T(8,128)(2,1)S(1)} %collective-permute-done.12.refs_1_), channel_id=1, source_target_pairs={{0,1},{1,0},{2,3},{3,2},{4,5},{5,4},{6,7},{7,6},{8,9},{9,8},{10,11... | collective-permute-start | bytes 983048 | tf_op jit(solution)/shard_map/ppermute | solution.py:275
  117.5 22.8 %copy-start = (s32[256]{0:T(256)S(1)}, s32[256]{0:T(256)}, u32[]{:S(2)}) copy-start(s32[256]{0:T(256)} %param.10) | copy-start | bytes 3076
  132.7 2.7 %collective-permute-start.17 = (bf16[8,256,256]{2,1,0:T(8,128)(2,1)S(1)}, bf16[8,256,256]{2,1,0:T(8,128)(2,1)S(1)}, u32[]{:S(2)}, u32[]{:S(2)}) collective-permute-start(bf16[8,256,256]{2,1,0:T(8,128)(2,1)S(1)} %get-tuple-element.63), channel_id=1, source_target_pairs={{0,1},{1,0},{2,3},{3,2},{4,5},{5,4},{6,7},{7,6},{8,9},{9,8},{10,11... | collective-permute-start | bytes 3145736 | tf_op jit(solution)/shard_map/ppermute | solution.py:275
  136.7 29.8 %all-to-all-start.1 = ((bf16[8,256,256]{2,1,0:T(8,128)(2,1)}), bf16[8,256,256]{2,1,0:T(8,128)(2,1)S(1)}, u32[]{:S(2)}, u32[]{:S(2)}) async-start(bf16[8,256,256]{2,1,0:T(8,128)(2,1)} %add_convert_fusion), calls=%async_computation.1 | async-start | bytes 2097152 | tf_op jit(solution)/shard_map/all_to_all | solution.py:300

commit v3 on v2

--- a/solution.py
+++ b/solution.py
@@ -42,40 +42,56 @@
     held = None if first else take(2)
     t_out, s_out = take(2)
     tops, stats = take(2) if len(refs) > 2 else (None, None)
-    xt, xs = take(2)
-    run = take(1)[0] if tops is not None else None
+    xt, xs, run = take(3) if tops is not None else (None, None, None)
     step, steps = pl.program_id(0), pl.num_programs(0)
     vocab, rows = t_out.shape
 
-    @pl.when(step == 0)
-    def _():
-        for shard in range(count):
-            at = 0
-            for part in parts[shard * pieces : (shard + 1) * pieces]:
-                span = pl.ds(at, part.shape[0])
-                xt[shard, span, :] = part[:, :dt]
-                xs[shard, span, :] = part[:, dt:]
-                at += part.shape[0]
-        if run is not None:
+    if run is not None:
+
+        @pl.when(step == 0)
+        def _():
+            for shard in range(count):
+                at = 0
+                for part in parts[shard * pieces : (shard + 1) * pieces]:
+                    span = pl.ds(at, part.shape[0])
+                    xt[shard, span, :] = part[:, :dt]
+                    xs[shard, span, :] = part[:, dt:]
+                    at += part.shape[0]
             run[...] = jnp.zeros_like(run)
             run[0:1, :] = jnp.full((1, rows), -jnp.inf, f32)
             run[3:4, :] = jnp.full((1, rows), -jnp.inf, f32)
 
     def multiply(size):
         here = pl.ds(pl.multiple_of(step * block, 8), size)
+        if run is None:
+            at = 0
+            for piece in range(pieces):
+                width = parts[piece].shape[0]
+                cols = pl.ds(at, width)
+                at += width
+                for out, prior, weight, low, high in (
+                    (t_out, 0, wt, 0, dt),
+                    (s_out, 1, ws, dt, parts[piece].shape[1]),
+                ):
+                    value = None if first else held[prior][here, cols]
+                    for shard in range(count):
+                        add = lax.dot_general(
+                            weight[shard][:size],
+                            parts[shard * pieces + piece][:, low:high],
+                            NT,
+                            preferred_element_type=f32,
+                        )
+                        value = add if value is None else value + add
+                    out[here, cols] = value
+            return
         t = s = None
         for shard in range(count):
             t_add = lax.dot_general(wt[shard][:size], xt[shard], NT, preferred_element_type=f32)
             s_add = lax.dot_general(ws[shard][:size], xs[shard], NT, preferred_element_type=f32)
             t = t_add if t is None else t + t_add
             s = s_add if s is None else s + s_add
-        if not first:
-            t = t + held[0][here, :]
-            s = s + held[1][here, :]
-        if run is None:
-            t_out[here, :] = t
-            s_out[here, :] = s
-            return
+        t = t + held[0][here, :]
+        s = s + held[1][here, :]
         t_top = jnp.max(t, axis=0, keepdims=True)
         s_top = jnp.max(s, axis=0, keepdims=True)
         t_exp = jnp.exp(t - t_top)
@@ -125,26 +141,24 @@
     block = min(block, vocab)
     blocks = pl.cdiv(vocab, block)
     parts = [part for shard in shards for part in shard]
-    in_specs = [
-        pl.BlockSpec(part.shape, lambda j, o: (0, 0), pipeline_mode=pl.Buffered(1))
-        for part in parts
-    ]
+    in_specs = [WHOLE] * len(parts)
     for width in (dt, ds):
         in_specs += [
             pl.BlockSpec((block, width), lambda j, o, pick=pick: (j, o[pick])) for pick in picks
         ]
-    args = parts + [wt] * count + [ws] * count
+    args = [pinned(part) for part in parts] + [wt] * count + [ws] * count
     aliases = {}
     if held is not None:
         aliases = {1 + len(args): 0, 2 + len(args): 1}
         in_specs += [WHOLE, WHOLE]
         args += [pinned(array) for array in held]
     out_shape, out_specs = [pltpu.VMEM((vocab, rows), f32)] * 2, [WHOLE, WHOLE]
-    scratch = [pltpu.VMEM((count, rows, dt), bf16), pltpu.VMEM((count, rows, ds), bf16)]
+    scratch = []
     if last:
         for shape in ((blocks, 8, rows), (copies, 8, rows)):
             out_shape.append(jax.ShapeDtypeStruct(shape, f32))
             out_specs.append(pl.BlockSpec(shape, lambda j, o: (0, 0, 0)))
+        scratch += [pltpu.VMEM((count, rows, width), bf16) for width in (dt, ds)]
         scratch.append(pltpu.VMEM((8, rows), f32))
     return pl.pallas_call(
         functools.partial(stage_kernel, count, pieces, dt, held is None, block),
@@ -297,10 +311,15 @@
     kl, own, other = grad_partial(offs, every, tops, t_exp, s_exp, ws, count)
     rows = teacher_hidden.shape[0]
     partial = (own + sibling(other).astype(f32)).astype(bf16)
-    shares = lax.all_to_all(partial, "vocab", 0, 0, tiled=True)
+    here = lax.axis_index("vocab")
+    total = lax.dynamic_index_in_dim(partial, here, 0, False).astype(f32)
+    wing = count // 2
+    for shift in list(range(wing, count)) + list(range(1, wing)):
+        pairs = [(chip, (chip + shift) % count) for chip in range(count)]
+        share = lax.dynamic_index_in_dim(partial, (here + shift) % count, 0, False)
+        total = total + lax.ppermute(share, "vocab", pairs).astype(f32)
     mask = loss_scale * loss_mask.astype(f32)
-    grad = mask[:, None] * jnp.sum(shares.astype(f32), axis=0)
-    return (kl[0, :rows], grad.astype(bf16))
+    return (kl[0, :rows], (mask[:, None] * total).astype(bf16))
 
 
 def gathered(teacher_hidden, teacher_weight, student_hidden, student_weight, loss_mask):

time: 168 us -> 164 us (0.976)
  waiting for transfers between devices: 37 us -> 26.1 us
  starting transfers between devices: 15.2 us -> 22.6 us
    all_to_all x1 -> x0, waiting for transfers between devices: 25.7 us -> none  [ringed(): shares = lax.all_to_all(partial, 'vocab', 0, 0, tiled=True)]
    ppermute x0 -> x7, waiting for transfers between devices: none -> 14.7 us  [ringed(): total = total + lax.ppermute(share, 'vocab', pairs).astype(f32)]
    ppermute x0 -> x7, starting transfers between devices: none -> 11 us  [ringed(): total = total + lax.ppermute(share, 'vocab', pairs).astype(f32)]
    all_to_all x1 -> x0, starting transfers between devices: 3.56 us -> none  [ringed(): shares = lax.all_to_all(partial, 'vocab', 0, 0, tiled=True)]
  transfers between devices with their start and end apart: 19 -> 25, of which waited for: 9 -> 11; matrix products, arithmetic and copies ran while one was open for 1% -> 1% of each run, Pallas kernels for 38% -> 39%
where the time goes in v3:
time: 164 us; the launch traced here: 163 us
  Pallas kernels  93 us (57%)
  waiting for transfers between devices  26.1 us (16%)
  starting transfers between devices  22.6 us (14%)
  blocking collectives  14.8 us (9%)
  local copies, waits for them, and re-layouts  3.38 us (2%)
  other arithmetic  2.35 us (1%)
    pallas_call x5, Pallas kernels, stage(): pl.pallas_call(functools.partial(stage_kernel, count, pieces, dt, held is...  77.8 us
    pallas_call x1, Pallas kernels, grad_partial(): pl.pallas_call(functools.partial(grad_kernel, block), grid_spec=pltpu.Pre...  15.2 us
    all_to_all x1, blocking collectives, ringed(): every = lax.all_to_all(stats, ('vocab', 'tok'), 0, 0, tiled=True)  14.8 us
    ppermute x7, waiting for transfers between devices, ringed(): total = total + lax.ppermute(share, 'vocab', pairs).astype(f32)  14.7 us
    ppermute x7, starting transfers between devices, ringed(): total = total + lax.ppermute(share, 'vocab', pairs).astype(f32)  11 us
    ppermute x4, starting transfers between devices, ringed(): next_low = lax.ppermute(from_low[:half] if final else from_low, 'vocab', up)  7.51 us
    ppermute x10, waiting for transfers between devices, sibling(): return lax.ppermute(array, 'tok', SWAP)  5.65 us
    ppermute x4, waiting for transfers between devices, ringed(): next_low = lax.ppermute(from_low[:half] if final else from_low, 'vocab', up)  4.25 us
  transfers between devices with their start and end apart: 25, of which 11 were waited for; matrix products, arithmetic and copies ran while one was open for 1% of the time, Pallas kernels for 39%

profile of v3, /device:TPU:0, one launch (start us, length us, event | category | flops | bytes accessed | tf_op | source)
XLA Modules:
  0.0 163.1 jit_solution(1392500263388913767)
XLA Ops:
  3.1 2.6 %collective-permute-start = (bf16[256,1280]{1,0:T(8,128)(2,1)S(1)}, bf16[256,1280]{1,0:T(8,128)(2,1)S(1)}, u32[]{:S(2)}, u32[]{:S(2)}) collective-permute-start(bf16[256,1280]{1,0:T(8,128)(2,1)S(1)} %constant_dynamic-update-slice_fusion.refs_0_), channel_id=1, source_target_pairs={{0,4},{4,8},{8,12},{12,14},{14,10},{10,6},{6,2},{2,0},{1,5},{5,9},... | collective-permute-start | bytes 1966088 | tf_op jit(solution)/shard_map/ppermute | solution.py:299
  6.6 10.2 %stage.4 = (f32[4752,512]{1,0:T(8,128)S(1)}, f32[4752,512]{1,0:T(8,128)S(1)}) custom-call(s32[9]{0:T(128)S(1)} %pad_add_fusion.off_ref, bf16[256,1280]{1,0:T(8,128)(2,1)S(1)} %constant_dynamic-update-slice_fusion.refs_0_, bf16[256,1280]{1,0:T(8,128)(2,1)S(1)} %collective-permute-done.2.refs_1_, bf16[4752,8192]{1,0:T(8,128)(2,1)} %bitcast.2.refs_2_.refs_4_.refs_5_, ...), custom_call_target="tpu_custom_call" | custom-call | flops 6228541440 | bytes 12165120 | tf_op jit(solution)/shard_map/stage/pallas_call | solution.py:163
  16.8 4.2 %collective-permute-done.refs_0_ = bf16[256,1280]{1,0:T(8,128)(2,1)S(1)} collective-permute-done((bf16[256,1280]{1,0:T(8,128)(2,1)S(1)}, bf16[256,1280]{1,0:T(8,128)(2,1)S(1)}, u32[]{:S(2)}, u32[]{:S(2)}) %collective-permute-start) | collective-permute-done | bytes 655392 | tf_op jit(solution)/shard_map/ppermute | solution.py:299
  21.1 1.5 collective-permute-done.1.refs_2_
  23.1 1.6 collective-permute-start.3
  25.6 17.6 %stage.5 = (f32[4752,512]{1,0:T(8,128)S(1)}, f32[4752,512]{1,0:T(8,128)S(1)}) custom-call(s32[9]{0:T(128)S(1)} %pad_add_fusion.off_ref, bf16[256,1280]{1,0:T(8,128)(2,1)S(1)} %collective-permute-done.refs_0_, bf16[256,1280]{1,0:T(8,128)(2,1)S(1)} %collective-permute-done.5.refs_1_, ...), custom_call_target="tpu_custom_call", output_to_operand_aliasing={{0}: (9, {}), {1}: (10, {})} | custom-call | flops 12457082880 | bytes 24330240 | tf_op jit(solution)/shard_map/stage/pallas_call | solution.py:163
  43.8 1.6 collective-permute-start.7
  46.4 17.6 %stage.6 = (f32[4752,512]{1,0:T(8,128)S(1)}, f32[4752,512]{1,0:T(8,128)S(1)}) custom-call(s32[9]{0:T(128)S(1)} %pad_add_fusion.off_ref, bf16[256,1280]{1,0:T(8,128)(2,1)S(1)} %collective-permute-done.3.refs_0_, bf16[256,1280]{1,0:T(8,128)(2,1)S(1)} %collective-permute-done.9.refs_1_, ...), custom_call_target="tpu_custom_call", output_to_operand_aliasing={{0}: (9, {}), {1}: (10, {})} | custom-call | flops 12457082880 | bytes 24330240 | tf_op jit(solution)/shard_map/stage/pallas_call | solution.py:163
  64.7 1.7 %collective-permute-start.11 = (bf16[128,1280]{1,0:T(8,128)(2,1)S(1)}, bf16[128,1280]{1,0:T(8,128)(2,1)S(1)}, u32[]{:S(2)}, u32[]{:S(2)}) collective-permute-start(bf16[128,1280]{1,0:T(8,128)(2,1)S(1)} %slice.9), channel_id=1, source_target_pairs={{0,4},{4,8},{8,12},{12,14},{14,10},{10,6},{6,2},{2,0},{1,5},{5,9},... | collective-permute-start | bytes 983048 | tf_op jit(solution)/shard_map/ppermute | solution.py:299
  67.1 17.6 %stage.7 = (f32[4752,512]{1,0:T(8,128)S(1)}, f32[4752,512]{1,0:T(8,128)S(1)}) custom-call(s32[9]{0:T(128)S(1)} %pad_add_fusion.off_ref, bf16[256,1280]{1,0:T(8,128)(2,1)S(1)} %collective-permute-done.7.refs_0_, bf16[256,1280]{1,0:T(8,128)(2,1)S(1)} %collective-permute-done.13.refs_1_, ...), custom_call_target="tpu_custom_call", output_to_operand_aliasing={{0}: (9, {}), {1}: (10, {})} | custom-call | flops 12457082880 | bytes 24330240 | tf_op jit(solution)/shard_map/stage/pallas_call | solution.py:163
  85.3 1.1 collective-permute-done.15.refs_2_
  86.9 14.7 %stage_last.1 = (f32[4752,512]{1,0:T(8,128)S(1)}, f32[4752,512]{1,0:T(8,128)S(1)}, f32[5,8,512]{2,1,0:T(8,128)S(1)}, f32[16,8,512]{2,1,0:T(8,128)S(1)}) custom-call(s32[9]{0:T(128)S(1)} %pad_add_fusion.off_ref, bf16[128,1280]{1,0:T(8,128)(2,1)S(1)} %collective-permute-done.11.refs_0_, ...), custom_call_target="tpu_custom_call", output_to_operand_aliasing={{0}: (7, {}), {1}: (8, {})} | custom-call | flops 6228541440 | bytes 12165120 | tf_op jit(solution)/shard_map/stage_last/pallas_call | solution.py:163
  101.6 14.8 %all_to_all.5.stats = f32[16,8,512]{2,1,0:T(8,128)S(1)} all-to-all(f32[16,8,512]{2,1,0:T(8,128)S(1)} %get-tuple-element.57), channel_id=1, replica_groups=mesh['groups'=2,'vocab'=8,'tok'=2] {'vocab','tok'}, dimensions={0} | all-to-all | bytes 524288 | tf_op jit(solution)/shard_map/all_to_all | solution.py:310
  116.4 15.2 %grad.1 = (f32[1,512]{1,0:T(1,128)S(1)}, f32[8,256,256]{2,1,0:T(8,128)S(1)}, bf16[8,256,256]{2,1,0:T(8,128)(2,1)S(1)}) custom-call(s32[9]{0:T(128)S(1)} %pad_add_fusion.off_ref, f32[16,8,512]{2,1,0:T(8,128)S(1)} %all_to_all.5.stats, f32[5,8,512]{2,1,0:T(8,128)S(1)} %get-tuple-element.58.tops, f32[4752,512]{1,0:T(8,128)S(1)} %get-tuple-element.59.t_exp, ...), custom_call_target="tpu_custom_call" | custom-call | flops 9965666304 | bytes 19464192 | tf_op jit(solution)/shard_map/grad/pallas_call | solution.py:237
  131.8 2.7 %collective-permute-done.17 = bf16[8,256,256]{2,1,0:T(8,128)(2,1)} collective-permute-done((bf16[8,256,256]{2,1,0:T(8,128)(2,1)S(1)}, bf16[8,256,256]{2,1,0:T(8,128)(2,1)}, u32[]{:S(2)}, u32[]{:S(2)}) %collective-permute-start.17) | collective-permute-done | bytes 1048608 | tf_op jit(solution)/shard_map/ppermute | solution.py:289
  134.5 1.5 add_convert_fusion
  136.1 1.1 collective-permute-start.18
  137.2 1.5 collective-permute-start.19
  138.7 2.0 %collective-permute-start.20 = (bf16[256,256]{1,0:T(8,128)(2,1)S(1)}, bf16[256,256]{1,0:T(8,128)(2,1)S(1)}, u32[]{:S(2)}, u32[]{:S(2)}) collective-permute-start(bf16[256,256]{1,0:T(8,128)(2,1)S(1)} %get-tuple-element.69), channel_id=1, source_target_pairs={{0,12},{2,14},{4,0},{6,2},{8,4},{10,6},{12,8},{14,10},{1,13},{3,15... | collective-permute-start | bytes 393224 | tf_op jit(solution)/shard_map/ppermute | solution.py:320
  141.5 1.2 collective-permute-start.22
  142.7 5.7 %collective-permute-done.18 = bf16[256,256]{1,0:T(8,128)(2,1)S(1)} collective-permute-done((bf16[256,256]{1,0:T(8,128)(2,1)S(1)}, bf16[256,256]{1,0:T(8,128)(2,1)S(1)}, u32[]{:S(2)}, u32[]{:S(2)}) %collective-permute-start.18) | collective-permute-done | bytes 131104 | tf_op jit(solution)/shard_map/ppermute | solution.py:320
  148.4 4.4 %collective-permute-start.23 = (bf16[256,256]{1,0:T(8,128)(2,1)S(1)}, bf16[256,256]{1,0:T(8,128)(2,1)S(1)}, u32[]{:S(2)}, u32[]{:S(2)}) collective-permute-start(bf16[256,256]{1,0:T(8,128)(2,1)S(1)} %get-tuple-element.66), channel_id=1, source_target_pairs={{0,4},{2,6},{4,8},{6,10},{8,12},{10,14},{12,0},{14,2},{1,5},{3,7},... | collective-permute-start | bytes 393224 | tf_op jit(solution)/shard_map/ppermute | solution.py:320
  153.3 6.4 %collective-permute-done.23 = bf16[256,256]{1,0:T(8,128)(2,1)S(1)} collective-permute-done((bf16[256,256]{1,0:T(8,128)(2,1)S(1)}, bf16[256,256]{1,0:T(8,128)(2,1)S(1)}, u32[]{:S(2)}, u32[]{:S(2)}) %collective-permute-start.23) | collective-permute-done | bytes 131104 | tf_op jit(solution)/shard_map/ppermute | solution.py:320
  159.7 2.6 %collective-permute-done.24 = bf16[256,256]{1,0:T(8,128)(2,1)S(1)} collective-permute-done((bf16[256,256]{1,0:T(8,128)(2,1)S(1)}, bf16[256,256]{1,0:T(8,128)(2,1)S(1)}, u32[]{:S(2)}, u32[]{:S(2)}) %collective-permute-start.24) | collective-permute-done | bytes 131104 | tf_op jit(solution)/shard_map/ppermute | solution.py:320
  (46 shorter events, 11.1 us)
Async XLA Ops:
  2.6 4.0 %collective-permute-start.2 = (bf16[256,1280]{1,0:T(8,128)(2,1)S(1)}, bf16[256,1280]{1,0:T(8,128)(2,1)S(1)}, u32[]{:S(2)}, u32[]{:S(2)}) collective-permute-start(bf16[256,1280]{1,0:T(8,128)(2,1)S(1)} %constant_dynamic-update-slice_fusion.refs_0_), channel_id=1, source_target_pairs={{0,1},{1,0},{2,3},{3,2},{4,5},{5,4},{6,7},{7,6},{8,9},{9,8},{10,11... | collective-permute-start | bytes 1966088 | tf_op jit(solution)/shard_map/ppermute | solution.py:289
  3.1 17.9 %collective-permute-start = (bf16[256,1280]{1,0:T(8,128)(2,1)S(1)}, bf16[256,1280]{1,0:T(8,128)(2,1)S(1)}, u32[]{:S(2)}, u32[]{:S(2)}) collective-permute-start(bf16[256,1280]{1,0:T(8,128)(2,1)S(1)} %constant_dynamic-update-slice_fusion.refs_0_), channel_id=1, source_target_pairs={{0,4},{4,8},{8,12},{12,14},{14,10},{10,6},{6,2},{2,0},{1,5},{5,9},... | collective-permute-start | bytes 1966088 | tf_op jit(solution)/shard_map/ppermute | solution.py:299
  5.8 16.8 %collective-permute-start.1 = (bf16[256,1280]{1,0:T(8,128)(2,1)S(1)}, bf16[256,1280]{1,0:T(8,128)(2,1)S(1)}, u32[]{:S(2)}, u32[]{:S(2)}) collective-permute-start(bf16[256,1280]{1,0:T(8,128)(2,1)S(1)} %constant_dynamic-update-slice_fusion.refs_0_), channel_id=1, source_target_pairs={{4,0},{8,4},{12,8},{14,12},{10,14},{6,10},{2,6},{0,2},{5,1},{9,5},... | collective-permute-start | bytes 1966088 | tf_op jit(solution)/shard_map/ppermute | solution.py:300
  22.6 2.5 %collective-permute-start.5 = (bf16[256,1280]{1,0:T(8,128)(2,1)S(1)}, bf16[256,1280]{1,0:T(8,128)(2,1)S(1)}, u32[]{:S(2)}, u32[]{:S(2)}) collective-permute-start(bf16[256,1280]{1,0:T(8,128)(2,1)S(1)} %collective-permute-done.refs_0_), channel_id=1, source_target_pairs={{0,1},{1,0},{2,3},{3,2},{4,5},{5,4},{6,7},{7,6},{8,9},{9,8},{10,11... | collective-permute-start | bytes 1966088 | tf_op jit(solution)/shard_map/ppermute | solution.py:289
  22.6 3.0 %collective-permute-start.6 = (bf16[256,1280]{1,0:T(8,128)(2,1)S(1)}, bf16[256,1280]{1,0:T(8,128)(2,1)S(1)}, u32[]{:S(2)}, u32[]{:S(2)}) collective-permute-start(bf16[256,1280]{1,0:T(8,128)(2,1)S(1)} %collective-permute-done.1.refs_2_), channel_id=1, source_target_pairs={{0,1},{1,0},{2,3},{3,2},{4,5},{5,4},{6,7},{7,6},{8,9},{9,8},{10,11... | collective-permute-start | bytes 1966088 | tf_op jit(solution)/shard_map/ppermute | solution.py:289
  23.1 20.1 %collective-permute-start.3 = (bf16[256,1280]{1,0:T(8,128)(2,1)S(1)}, bf16[256,1280]{1,0:T(8,128)(2,1)S(1)}, u32[]{:S(2)}, u32[]{:S(2)}) collective-permute-start(bf16[256,1280]{1,0:T(8,128)(2,1)S(1)} %collective-permute-done.refs_0_), channel_id=1, source_target_pairs={{0,4},{4,8},{8,12},{12,14},{14,10},{10,6},{6,2},{2,0},{1,5},{5,9},... | collective-permute-start | bytes 1966088 | tf_op jit(solution)/shard_map/ppermute | solution.py:299
  24.7 18.6 %collective-permute-start.4 = (bf16[256,1280]{1,0:T(8,128)(2,1)S(1)}, bf16[256,1280]{1,0:T(8,128)(2,1)S(1)}, u32[]{:S(2)}, u32[]{:S(2)}) collective-permute-start(bf16[256,1280]{1,0:T(8,128)(2,1)S(1)} %collective-permute-done.1.refs_2_), channel_id=1, source_target_pairs={{4,0},{8,4},{12,8},{14,12},{10,14},{6,10},{2,6},{0,2},{5,1},{9,5},... | collective-permute-start | bytes 1966088 | tf_op jit(solution)/shard_map/ppermute | solution.py:300
  43.3 2.6 %collective-permute-start.10 = (bf16[256,1280]{1,0:T(8,128)(2,1)S(1)}, bf16[256,1280]{1,0:T(8,128)(2,1)S(1)}, u32[]{:S(2)}, u32[]{:S(2)}) collective-permute-start(bf16[256,1280]{1,0:T(8,128)(2,1)S(1)} %collective-permute-done.4.refs_2_), channel_id=1, source_target_pairs={{0,1},{1,0},{2,3},{3,2},{4,5},{5,4},{6,7},{7,6},{8,9},{9,8},{10,11... | collective-permute-start | bytes 1966088 | tf_op jit(solution)/shard_map/ppermute | solution.py:289
  43.4 2.9 %collective-permute-start.9 = (bf16[256,1280]{1,0:T(8,128)(2,1)S(1)}, bf16[256,1280]{1,0:T(8,128)(2,1)S(1)}, u32[]{:S(2)}, u32[]{:S(2)}) collective-permute-start(bf16[256,1280]{1,0:T(8,128)(2,1)S(1)} %collective-permute-done.3.refs_0_), channel_id=1, source_target_pairs={{0,1},{1,0},{2,3},{3,2},{4,5},{5,4},{6,7},{7,6},{8,9},{9,8},{10,11... | collective-permute-start | bytes 1966088 | tf_op jit(solution)/shard_map/ppermute | solution.py:289
  43.8 20.2 %collective-permute-start.7 = (bf16[256,1280]{1,0:T(8,128)(2,1)S(1)}, bf16[256,1280]{1,0:T(8,128)(2,1)S(1)}, u32[]{:S(2)}, u32[]{:S(2)}) collective-permute-start(bf16[256,1280]{1,0:T(8,128)(2,1)S(1)} %collective-permute-done.3.refs_0_), channel_id=1, source_target_pairs={{0,4},{4,8},{8,12},{12,14},{14,10},{10,6},{6,2},{2,0},{1,5},{5,9},... | collective-permute-start | bytes 1966088 | tf_op jit(solution)/shard_map/ppermute | solution.py:299
  45.5 18.6 %collective-permute-start.8 = (bf16[256,1280]{1,0:T(8,128)(2,1)S(1)}, bf16[256,1280]{1,0:T(8,128)(2,1)S(1)}, u32[]{:S(2)}, u32[]{:S(2)}) collective-permute-start(bf16[256,1280]{1,0:T(8,128)(2,1)S(1)} %collective-permute-done.4.refs_2_), channel_id=1, source_target_pairs={{4,0},{8,4},{12,8},{14,12},{10,14},{6,10},{2,6},{0,2},{5,1},{9,5},... | collective-permute-start | bytes 1966088 | tf_op jit(solution)/shard_map/ppermute | solution.py:300
  64.0 2.7 %collective-permute-start.13 = (bf16[256,1280]{1,0:T(8,128)(2,1)S(1)}, bf16[256,1280]{1,0:T(8,128)(2,1)S(1)}, u32[]{:S(2)}, u32[]{:S(2)}) collective-permute-start(bf16[256,1280]{1,0:T(8,128)(2,1)S(1)} %collective-permute-done.7.refs_0_), channel_id=1, source_target_pairs={{0,1},{1,0},{2,3},{3,2},{4,5},{5,4},{6,7},{7,6},{8,9},{9,8},{10,11... | collective-permute-start | bytes 1966088 | tf_op jit(solution)/shard_map/ppermute | solution.py:289
  64.2 2.9 %collective-permute-start.14 = (bf16[256,1280]{1,0:T(8,128)(2,1)S(1)}, bf16[256,1280]{1,0:T(8,128)(2,1)S(1)}, u32[]{:S(2)}, u32[]{:S(2)}) collective-permute-start(bf16[256,1280]{1,0:T(8,128)(2,1)S(1)} %collective-permute-done.8.refs_2_), channel_id=1, source_target_pairs={{0,1},{1,0},{2,3},{3,2},{4,5},{5,4},{6,7},{7,6},{8,9},{9,8},{10,11... | collective-permute-start | bytes 1966088 | tf_op jit(solution)/shard_map/ppermute | solution.py:289
  64.7 20.1 %collective-permute-start.11 = (bf16[128,1280]{1,0:T(8,128)(2,1)S(1)}, bf16[128,1280]{1,0:T(8,128)(2,1)S(1)}, u32[]{:S(2)}, u32[]{:S(2)}) collective-permute-start(bf16[128,1280]{1,0:T(8,128)(2,1)S(1)} %slice.9), channel_id=1, source_target_pairs={{0,4},{4,8},{8,12},{12,14},{14,10},{10,6},{6,2},{2,0},{1,5},{5,9},... | collective-permute-start | bytes 983048 | tf_op jit(solution)/shard_map/ppermute | solution.py:299
  66.3 18.4 %collective-permute-start.12 = (bf16[128,1280]{1,0:T(8,128)(2,1)S(1)}, bf16[128,1280]{1,0:T(8,128)(2,1)S(1)}, u32[]{:S(2)}, u32[]{:S(2)}) collective-permute-start(bf16[128,1280]{1,0:T(8,128)(2,1)S(1)} %slice.10), channel_id=1, source_target_pairs={{4,0},{8,4},{12,8},{14,12},{10,14},{6,10},{2,6},{0,2},{5,1},{9,5},... | collective-permute-start | bytes 983048 | tf_op jit(solution)/shard_map/ppermute | solution.py:300
  85.0 1.9 %collective-permute-start.16 = (bf16[128,1280]{1,0:T(8,128)(2,1)S(1)}, bf16[128,1280]{1,0:T(8,128)(2,1)S(1)}, u32[]{:S(2)}, u32[]{:S(2)}) collective-permute-start(bf16[128,1280]{1,0:T(8,128)(2,1)S(1)} %collective-permute-done.12.refs_1_), channel_id=1, source_target_pairs={{0,1},{1,0},{2,3},{3,2},{4,5},{5,4},{6,7},{7,6},{8,9},{9,8},{10,11... | collective-permute-start | bytes 983048 | tf_op jit(solution)/shard_map/ppermute | solution.py:289
  131.6 2.9 %collective-permute-start.17 = (bf16[8,256,256]{2,1,0:T(8,128)(2,1)S(1)}, bf16[8,256,256]{2,1,0:T(8,128)(2,1)}, u32[]{:S(2)}, u32[]{:S(2)}) collective-permute-start(bf16[8,256,256]{2,1,0:T(8,128)(2,1)S(1)} %get-tuple-element.63), channel_id=1, source_target_pairs={{0,1},{1,0},{2,3},{3,2},{4,5},{5,4},{6,7},{7,6},{8,9},{9,8},{10,11... | collective-permute-start | bytes 3145736 | tf_op jit(solution)/shard_map/ppermute | solution.py:289
  136.1 12.3 %collective-permute-start.18 = (bf16[256,256]{1,0:T(8,128)(2,1)S(1)}, bf16[256,256]{1,0:T(8,128)(2,1)S(1)}, u32[]{:S(2)}, u32[]{:S(2)}) collective-permute-start(bf16[256,256]{1,0:T(8,128)(2,1)S(1)} %get-tuple-element.64), channel_id=1, source_target_pairs={{0,8},{2,10},{4,12},{6,14},{8,0},{10,2},{12,4},{14,6},{1,9},{3,11}... | collective-permute-start | bytes 393224 | tf_op jit(solution)/shard_map/ppermute | solution.py:320
  137.2 15.6 %collective-permute-start.19 = (bf16[256,256]{1,0:T(8,128)(2,1)S(1)}, bf16[256,256]{1,0:T(8,128)(2,1)S(1)}, u32[]{:S(2)}, u32[]{:S(2)}) collective-permute-start(bf16[256,256]{1,0:T(8,128)(2,1)S(1)} %get-tuple-element.70), channel_id=1, source_target_pairs={{0,10},{2,12},{4,14},{6,0},{8,2},{10,4},{12,6},{14,8},{1,11},{3,13... | collective-permute-start | bytes 393224 | tf_op jit(solution)/shard_map/ppermute | solution.py:320
  138.7 14.7 %collective-permute-start.20 = (bf16[256,256]{1,0:T(8,128)(2,1)S(1)}, bf16[256,256]{1,0:T(8,128)(2,1)S(1)}, u32[]{:S(2)}, u32[]{:S(2)}) collective-permute-start(bf16[256,256]{1,0:T(8,128)(2,1)S(1)} %get-tuple-element.69), channel_id=1, source_target_pairs={{0,12},{2,14},{4,0},{6,2},{8,4},{10,6},{12,8},{14,10},{1,13},{3,15... | collective-permute-start | bytes 393224 | tf_op jit(solution)/shard_map/ppermute | solution.py:320
  140.6 12.7 %collective-permute-start.21 = (bf16[256,256]{1,0:T(8,128)(2,1)S(1)}, bf16[256,256]{1,0:T(8,128)(2,1)S(1)}, u32[]{:S(2)}, u32[]{:S(2)}) collective-permute-start(bf16[256,256]{1,0:T(8,128)(2,1)S(1)} %get-tuple-element.68), channel_id=1, source_target_pairs={{0,14},{2,0},{4,2},{6,4},{8,6},{10,8},{12,10},{14,12},{1,15},{3,1}... | collective-permute-start | bytes 393224 | tf_op jit(solution)/shard_map/ppermute | solution.py:320
  141.5 11.8 %collective-permute-start.22 = (bf16[256,256]{1,0:T(8,128)(2,1)S(1)}, bf16[256,256]{1,0:T(8,128)(2,1)S(1)}, u32[]{:S(2)}, u32[]{:S(2)}) collective-permute-start(bf16[256,256]{1,0:T(8,128)(2,1)S(1)} %get-tuple-element.67), channel_id=1, source_target_pairs={{0,2},{2,4},{4,6},{6,8},{8,10},{10,12},{12,14},{14,0},{1,3},{3,5},... | collective-permute-start | bytes 393224 | tf_op jit(solution)/shard_map/ppermute | solution.py:320
  148.4 11.4 %collective-permute-start.23 = (bf16[256,256]{1,0:T(8,128)(2,1)S(1)}, bf16[256,256]{1,0:T(8,128)(2,1)S(1)}, u32[]{:S(2)}, u32[]{:S(2)}) collective-permute-start(bf16[256,256]{1,0:T(8,128)(2,1)S(1)} %get-tuple-element.66), channel_id=1, source_target_pairs={{0,4},{2,6},{4,8},{6,10},{8,12},{10,14},{12,0},{14,2},{1,5},{3,7},... | collective-permute-start | bytes 393224 | tf_op jit(solution)/shard_map/ppermute | solution.py:320
  152.7 9.6 %collective-permute-start.24 = (bf16[256,256]{1,0:T(8,128)(2,1)S(1)}, bf16[256,256]{1,0:T(8,128)(2,1)S(1)}, u32[]{:S(2)}, u32[]{:S(2)}) collective-permute-start(bf16[256,256]{1,0:T(8,128)(2,1)S(1)} %get-tuple-element.65), channel_id=1, source_target_pairs={{0,6},{2,8},{4,10},{6,12},{8,14},{10,0},{12,2},{14,4},{1,7},{3,9},... | collective-permute-start | bytes 393224 | tf_op jit(solution)/shard_map/ppermute | solution.py:320
  (2 other events, 38.0 us)

commit v4 on v3

--- a/solution.py
+++ b/solution.py
@@ -157,7 +157,7 @@
     if last:
         for shape in ((blocks, 8, rows), (copies, 8, rows)):
             out_shape.append(jax.ShapeDtypeStruct(shape, f32))
-            out_specs.append(pl.BlockSpec(shape, lambda j, o: (0, 0, 0)))
+            out_specs.append(WHOLE)
         scratch += [pltpu.VMEM((count, rows, width), bf16) for width in (dt, ds)]
         scratch.append(pltpu.VMEM((8, rows), f32))
     return pl.pallas_call(
@@ -229,28 +229,19 @@
     block = min(last_block, vocab)
     shares = (count, rows // 2, features // count)
 
-    def still(array):
-        return pl.BlockSpec(
-            array.shape, lambda j, o: (0, 0, 0), pipeline_mode=pl.Buffered(1)
-        )
-
     return pl.pallas_call(
         functools.partial(grad_kernel, block),
         grid_spec=pltpu.PrefetchScalarGridSpec(
             num_scalar_prefetch=1,
             grid=(pl.cdiv(vocab, block),),
             in_specs=[
-                still(stats),
-                still(tops),
+                WHOLE,
+                WHOLE,
                 WHOLE,
                 WHOLE,
                 pl.BlockSpec((block, features), lambda j, o: (j, 0)),
             ],
-            out_specs=[
-                pl.BlockSpec((1, rows), lambda j, o: (0, 0)),
-                pl.BlockSpec(shares, lambda j, o: (0, 0, 0)),
-                pl.BlockSpec(shares, lambda j, o: (0, 0, 0)),
-            ],
+            out_specs=[WHOLE, WHOLE, WHOLE],
             scratch_shapes=[pltpu.VMEM((rows, features), f32), pltpu.VMEM((8, rows), f32)],
         ),
         out_shape=[
@@ -310,14 +301,33 @@
     every = lax.all_to_all(stats, ("vocab", "tok"), 0, 0, tiled=True)
     kl, own, other = grad_partial(offs, every, tops, t_exp, s_exp, ws, count)
     rows = teacher_hidden.shape[0]
-    partial = (own + sibling(other).astype(f32)).astype(bf16)
-    here = lax.axis_index("vocab")
-    total = lax.dynamic_index_in_dim(partial, here, 0, False).astype(f32)
-    wing = count // 2
-    for shift in list(range(wing, count)) + list(range(1, wing)):
-        pairs = [(chip, (chip + shift) % count) for chip in range(count)]
-        share = lax.dynamic_index_in_dim(partial, (here + shift) % count, 0, False)
-        total = total + lax.ppermute(share, "vocab", pairs).astype(f32)
+    beside = sibling(other)
+    partial = (own + beside.astype(f32)).astype(bf16)
+    chip, units = lax.axis_index("vocab"), count // 2
+    middle = units // 2
+
+    def goal(c, shift, flip):
+        return (c // 2 + shift) % units * 2 + (c % 2 + flip) % 2
+
+    def share(shift, flip):
+        return lax.dynamic_index_in_dim(partial, goal(chip, shift, flip), 0, False)
+
+    def exact(shift, flip):
+        at = goal(chip, shift, flip)
+        pair = [lax.dynamic_index_in_dim(array, at, 0, False) for array in (own, beside)]
+        return pair[0] + pair[1].astype(f32)
+
+    def sent(value, shift, flip):
+        return lax.ppermute(value, "vocab", [(c, goal(c, shift, flip)) for c in range(count)])
+
+    near = sent(jnp.stack([share(0, 1), share(middle, 1)]), 0, 1).astype(f32)
+    total = exact(0, 0) + near[0]
+    for shift in range(1, units):
+        if shift != middle:
+            for flip in range(2):
+                total = total + sent(share(shift, flip), shift, flip).astype(f32)
+    merged = (exact(middle, 0) + near[1]).astype(bf16)
+    total = total + sent(merged, middle, 0).astype(f32)
     mask = loss_scale * loss_mask.astype(f32)
     return (kl[0, :rows], (mask[:, None] * total).astype(bf16))
 

time: 164 us -> 160 us (0.976)
  waiting for transfers between devices: 26.1 us -> 21.2 us
  other arithmetic: 2.35 us -> 4.26 us
    ppermute x7 -> x6, waiting for transfers between devices: 14.7 us -> 9.86 us  [sent(): lax.ppermute(value, 'vocab', [(c, goal(c, shift, flip)) for c in range(co...]
    ppermute x7 -> x6, starting transfers between devices: 11 us -> 10.1 us  [sent(): lax.ppermute(value, 'vocab', [(c, goal(c, shift, flip)) for c in range(co...]
  transfers between devices with their start and end apart: 25 -> 24, of which waited for: 11 -> 11; matrix products, arithmetic and copies ran while one was open for 1% -> 1% of each run, Pallas kernels for 39% -> 40%
where the time goes in v4:
time: 160 us; the launch traced here: 159 us
  Pallas kernels  93 us (58%)
  starting transfers between devices  21.7 us (14%)
  waiting for transfers between devices  21.2 us (13%)
  blocking collectives  14.8 us (9%)
  other arithmetic  4.26 us (3%)
  local copies, waits for them, and re-layouts  3.36 us (2%)
    pallas_call x5, Pallas kernels, stage(): pl.pallas_call(functools.partial(stage_kernel, count, pieces, dt, held is...  77.8 us
    pallas_call x1, Pallas kernels, grad_partial(): pl.pallas_call(functools.partial(grad_kernel, block), grid_spec=pltpu.Pre...  15.2 us
    all_to_all x1, blocking collectives, ringed(): every = lax.all_to_all(stats, ('vocab', 'tok'), 0, 0, tiled=True)  14.8 us
    ppermute x6, starting transfers between devices, sent(): lax.ppermute(value, 'vocab', [(c, goal(c, shift, flip)) for c in range(co...  10.1 us
    ppermute x6, waiting for transfers between devices, sent(): lax.ppermute(value, 'vocab', [(c, goal(c, shift, flip)) for c in range(co...  9.86 us
    ppermute x4, starting transfers between devices, ringed(): next_low = lax.ppermute(from_low[:half] if final else from_low, 'vocab', up)  7.51 us
    ppermute x10, waiting for transfers between devices, sibling(): return lax.ppermute(array, 'tok', SWAP)  5.61 us
    ppermute x4, waiting for transfers between devices, ringed(): next_low = lax.ppermute(from_low[:half] if final else from_low, 'vocab', up)  4.25 us
  transfers between devices with their start and end apart: 24, of which 11 were waited for; matrix products, arithmetic and copies ran while one was open for 1% of the time, Pallas kernels for 40%

profile of v4, /device:TPU:0, one launch (start us, length us, event | category | flops | bytes accessed | tf_op | source)
XLA Modules:
  0.0 159.3 jit_solution(1143080918144987074)
XLA Ops:
  3.1 2.6 %collective-permute-start = (bf16[256,1280]{1,0:T(8,128)(2,1)S(1)}, bf16[256,1280]{1,0:T(8,128)(2,1)S(1)}, u32[]{:S(2)}, u32[]{:S(2)}) collective-permute-start(bf16[256,1280]{1,0:T(8,128)(2,1)S(1)} %constant_dynamic-update-slice_fusion.refs_0_), channel_id=1, source_target_pairs={{0,4},{4,8},{8,12},{12,14},{14,10},{10,6},{6,2},{2,0},{1,5},{5,9},... | collective-permute-start | bytes 1966088 | tf_op jit(solution)/shard_map/ppermute | solution.py:290
  6.6 10.2 %stage.4 = (f32[4752,512]{1,0:T(8,128)S(1)}, f32[4752,512]{1,0:T(8,128)S(1)}) custom-call(s32[9]{0:T(128)S(1)} %pad_add_fusion.off_ref, bf16[256,1280]{1,0:T(8,128)(2,1)S(1)} %constant_dynamic-update-slice_fusion.refs_0_, bf16[256,1280]{1,0:T(8,128)(2,1)S(1)} %collective-permute-done.2.refs_1_, bf16[4752,8192]{1,0:T(8,128)(2,1)} %bitcast.2.refs_2_.refs_4_.refs_5_, ...), custom_call_target="tpu_custom_call" | custom-call | flops 6228541440 | bytes 12165120 | tf_op jit(solution)/shard_map/stage/pallas_call | solution.py:163
  16.8 4.2 %collective-permute-done.refs_0_ = bf16[256,1280]{1,0:T(8,128)(2,1)S(1)} collective-permute-done((bf16[256,1280]{1,0:T(8,128)(2,1)S(1)}, bf16[256,1280]{1,0:T(8,128)(2,1)S(1)}, u32[]{:S(2)}, u32[]{:S(2)}) %collective-permute-start) | collective-permute-done | bytes 655392 | tf_op jit(solution)/shard_map/ppermute | solution.py:290
  21.1 1.5 collective-permute-done.1.refs_2_
  23.1 1.6 collective-permute-start.3
  25.6 17.6 %stage.5 = (f32[4752,512]{1,0:T(8,128)S(1)}, f32[4752,512]{1,0:T(8,128)S(1)}) custom-call(s32[9]{0:T(128)S(1)} %pad_add_fusion.off_ref, bf16[256,1280]{1,0:T(8,128)(2,1)S(1)} %collective-permute-done.refs_0_, bf16[256,1280]{1,0:T(8,128)(2,1)S(1)} %collective-permute-done.5.refs_1_, ...), custom_call_target="tpu_custom_call", output_to_operand_aliasing={{0}: (9, {}), {1}: (10, {})} | custom-call | flops 12457082880 | bytes 24330240 | tf_op jit(solution)/shard_map/stage/pallas_call | solution.py:163
  43.8 1.6 %collective-permute-start.7 = (bf16[256,1280]{1,0:T(8,128)(2,1)S(1)}, bf16[256,1280]{1,0:T(8,128)(2,1)S(1)}, u32[]{:S(2)}, u32[]{:S(2)}) collective-permute-start(bf16[256,1280]{1,0:T(8,128)(2,1)S(1)} %collective-permute-done.3.refs_0_), channel_id=1, source_target_pairs={{0,4},{4,8},{8,12},{12,14},{14,10},{10,6},{6,2},{2,0},{1,5},{5,9},... | collective-permute-start | bytes 1966088 | tf_op jit(solution)/shard_map/ppermute | solution.py:290
  46.4 17.6 %stage.6 = (f32[4752,512]{1,0:T(8,128)S(1)}, f32[4752,512]{1,0:T(8,128)S(1)}) custom-call(s32[9]{0:T(128)S(1)} %pad_add_fusion.off_ref, bf16[256,1280]{1,0:T(8,128)(2,1)S(1)} %collective-permute-done.3.refs_0_, bf16[256,1280]{1,0:T(8,128)(2,1)S(1)} %collective-permute-done.9.refs_1_, ...), custom_call_target="tpu_custom_call", output_to_operand_aliasing={{0}: (9, {}), {1}: (10, {})} | custom-call | flops 12457082880 | bytes 24330240 | tf_op jit(solution)/shard_map/stage/pallas_call | solution.py:163
  64.7 1.7 %collective-permute-start.11 = (bf16[128,1280]{1,0:T(8,128)(2,1)S(1)}, bf16[128,1280]{1,0:T(8,128)(2,1)S(1)}, u32[]{:S(2)}, u32[]{:S(2)}) collective-permute-start(bf16[128,1280]{1,0:T(8,128)(2,1)S(1)} %slice.15), channel_id=1, source_target_pairs={{0,4},{4,8},{8,12},{12,14},{14,10},{10,6},{6,2},{2,0},{1,5},{5,9},... | collective-permute-start | bytes 983048 | tf_op jit(solution)/shard_map/ppermute | solution.py:290
  67.1 17.6 %stage.7 = (f32[4752,512]{1,0:T(8,128)S(1)}, f32[4752,512]{1,0:T(8,128)S(1)}) custom-call(s32[9]{0:T(128)S(1)} %pad_add_fusion.off_ref, bf16[256,1280]{1,0:T(8,128)(2,1)S(1)} %collective-permute-done.7.refs_0_, bf16[256,1280]{1,0:T(8,128)(2,1)S(1)} %collective-permute-done.13.refs_1_, ...), custom_call_target="tpu_custom_call", output_to_operand_aliasing={{0}: (9, {}), {1}: (10, {})} | custom-call | flops 12457082880 | bytes 24330240 | tf_op jit(solution)/shard_map/stage/pallas_call | solution.py:163
  85.3 1.1 collective-permute-done.15.refs_2_
  86.9 14.7 %stage_last.1 = (f32[4752,512]{1,0:T(8,128)S(1)}, f32[4752,512]{1,0:T(8,128)S(1)}, f32[5,8,512]{2,1,0:T(8,128)S(1)}, f32[16,8,512]{2,1,0:T(8,128)S(1)}) custom-call(s32[9]{0:T(128)S(1)} %pad_add_fusion.off_ref, bf16[128,1280]{1,0:T(8,128)(2,1)S(1)} %collective-permute-done.11.refs_0_, ...), custom_call_target="tpu_custom_call", output_to_operand_aliasing={{0}: (7, {}), {1}: (8, {})} | custom-call | flops 6228541440 | bytes 12165120 | tf_op jit(solution)/shard_map/stage_last/pallas_call | solution.py:163
  101.6 14.8 %all_to_all.5.stats = f32[16,8,512]{2,1,0:T(8,128)S(1)} all-to-all(f32[16,8,512]{2,1,0:T(8,128)S(1)} %get-tuple-element.57), channel_id=1, replica_groups=mesh['groups'=2,'vocab'=8,'tok'=2] {'vocab','tok'}, dimensions={0} | all-to-all | bytes 524288 | tf_op jit(solution)/shard_map/all_to_all | solution.py:301
  116.4 15.2 %grad.1 = (f32[1,512]{1,0:T(1,128)S(1)}, f32[8,256,256]{2,1,0:T(8,128)S(1)}, bf16[8,256,256]{2,1,0:T(8,128)(2,1)S(1)}) custom-call(s32[9]{0:T(128)S(1)} %pad_add_fusion.off_ref, f32[16,8,512]{2,1,0:T(8,128)S(1)} %all_to_all.5.stats, f32[5,8,512]{2,1,0:T(8,128)S(1)} %get-tuple-element.58.tops, f32[4752,512]{1,0:T(8,128)S(1)} %get-tuple-element.59.t_exp, ...), custom_call_target="tpu_custom_call" | custom-call | flops 9965666304 | bytes 19464192 | tf_op jit(solution)/shard_map/grad/pallas_call | solution.py:232
  131.9 2.6 %collective-permute-done.17 = bf16[8,256,256]{2,1,0:T(8,128)(2,1)} collective-permute-done((bf16[8,256,256]{2,1,0:T(8,128)(2,1)S(1)}, bf16[8,256,256]{2,1,0:T(8,128)(2,1)}, u32[]{:S(2)}, u32[]{:S(2)}) %collective-permute-start.17) | collective-permute-done | bytes 1048608 | tf_op jit(solution)/shard_map/ppermute | solution.py:280
  134.5 1.5 add_convert_fusion
  137.3 1.9 %collective-permute-start.20 = (bf16[256,256]{1,0:T(8,128)(2,1)S(1)}, bf16[256,256]{1,0:T(8,128)(2,1)S(1)}, u32[]{:S(2)}, u32[]{:S(2)}) collective-permute-start(bf16[256,256]{1,0:T(8,128)(2,1)S(1)} %get-tuple-element.67), channel_id=1, source_target_pairs={{0,6},{2,4},{4,10},{6,8},{8,14},{10,12},{12,2},{14,0},{1,7},{3,5},... | collective-permute-start | bytes 393224 | tf_op jit(solution)/shard_map/ppermute | solution.py:321
  139.2 2.5 %collective-permute-start.21 = (bf16[256,256]{1,0:T(8,128)(2,1)S(1)}, bf16[256,256]{1,0:T(8,128)(2,1)S(1)}, u32[]{:S(2)}, u32[]{:S(2)}) collective-permute-start(bf16[256,256]{1,0:T(8,128)(2,1)S(1)} %get-tuple-element.66), channel_id=1, source_target_pairs={{0,12},{2,14},{4,0},{6,2},{8,4},{10,6},{12,8},{14,10},{1,13},{3,15... | collective-permute-start | bytes 393224 | tf_op jit(solution)/shard_map/ppermute | solution.py:321
  141.8 1.3 collective-permute-start.22
  143.1 2.2 %collective-permute-done.18 = bf16[2,256,256]{2,1,0:T(8,128)(2,1)S(1)} collective-permute-done((bf16[2,256,256]{2,1,0:T(8,128)(2,1)S(1)}, bf16[2,256,256]{2,1,0:T(8,128)(2,1)S(1)}, u32[]{:S(2)}, u32[]{:S(2)}) %collective-permute-start.18) | collective-permute-done | bytes 262176 | tf_op jit(solution)/shard_map/ppermute | solution.py:321
  146.3 3.1 %collective-permute-start.23 = (bf16[256,256]{1,0:T(8,128)(2,1)S(1)}, bf16[256,256]{1,0:T(8,128)(2,1)S(1)}, u32[]{:S(2)}, u32[]{:S(2)}) collective-permute-start(bf16[256,256]{1,0:T(8,128)(2,1)S(1)} %fusion.9), channel_id=1, source_target_pairs={{0,8},{2,10},{4,12},{6,14},{8,0},{10,2},{12,4},{14,6},{1,9},{3,11}... | collective-permute-start | bytes 393224 | tf_op jit(solution)/shard_map/ppermute | solution.py:321
  150.0 2.2 %collective-permute-done.22 = bf16[256,256]{1,0:T(8,128)(2,1)S(1)} collective-permute-done((bf16[256,256]{1,0:T(8,128)(2,1)S(1)}, bf16[256,256]{1,0:T(8,128)(2,1)S(1)}, u32[]{:S(2)}, u32[]{:S(2)}) %collective-permute-start.22) | collective-permute-done | bytes 131104 | tf_op jit(solution)/shard_map/ppermute | solution.py:321
  152.2 5.5 %collective-permute-done.23 = bf16[256,256]{1,0:T(8,128)(2,1)S(1)} collective-permute-done((bf16[256,256]{1,0:T(8,128)(2,1)S(1)}, bf16[256,256]{1,0:T(8,128)(2,1)S(1)}, u32[]{:S(2)}, u32[]{:S(2)}) %collective-permute-start.23) | collective-permute-done | bytes 131104 | tf_op jit(solution)/shard_map/ppermute | solution.py:321
  157.6 1.7 %fusion.8 = bf16[256,256]{1,0:T(8,128)(2,1)} fusion(f32[2,256,256]{2,1,0:T(8,128)S(1)} %convert_element_type.48, bf16[256,256]{1,0:T(8,128)(2,1)S(1)} %collective-permute-done.23, bf16[256,256]{1,0:T(8,128)(2,1)S(1)} %collective-permute-done.22, bf16[256,256]{1,0:T(8,128)(2,1)S(1)} %collective-permute-done.21, ...), kind=kLoop, calls=%fused_computation.11 | loop fusion | flops 983040 | bytes 1442820 | tf_op jit(solution)/shard_map/convert_element_type | solution.py:332
  (47 shorter events, 11.7 us)
Async XLA Ops:
  2.6 4.0 %collective-permute-start.2 = (bf16[256,1280]{1,0:T(8,128)(2,1)S(1)}, bf16[256,1280]{1,0:T(8,128)(2,1)S(1)}, u32[]{:S(2)}, u32[]{:S(2)}) collective-permute-start(bf16[256,1280]{1,0:T(8,128)(2,1)S(1)} %constant_dynamic-update-slice_fusion.refs_0_), channel_id=1, source_target_pairs={{0,1},{1,0},{2,3},{3,2},{4,5},{5,4},{6,7},{7,6},{8,9},{9,8},{10,11... | collective-permute-start | bytes 1966088 | tf_op jit(solution)/shard_map/ppermute | solution.py:280
  3.1 17.9 %collective-permute-start = (bf16[256,1280]{1,0:T(8,128)(2,1)S(1)}, bf16[256,1280]{1,0:T(8,128)(2,1)S(1)}, u32[]{:S(2)}, u32[]{:S(2)}) collective-permute-start(bf16[256,1280]{1,0:T(8,128)(2,1)S(1)} %constant_dynamic-update-slice_fusion.refs_0_), channel_id=1, source_target_pairs={{0,4},{4,8},{8,12},{12,14},{14,10},{10,6},{6,2},{2,0},{1,5},{5,9},... | collective-permute-start | bytes 1966088 | tf_op jit(solution)/shard_map/ppermute | solution.py:290
  5.8 16.8 %collective-permute-start.1 = (bf16[256,1280]{1,0:T(8,128)(2,1)S(1)}, bf16[256,1280]{1,0:T(8,128)(2,1)S(1)}, u32[]{:S(2)}, u32[]{:S(2)}) collective-permute-start(bf16[256,1280]{1,0:T(8,128)(2,1)S(1)} %constant_dynamic-update-slice_fusion.refs_0_), channel_id=1, source_target_pairs={{4,0},{8,4},{12,8},{14,12},{10,14},{6,10},{2,6},{0,2},{5,1},{9,5},... | collective-permute-start | bytes 1966088 | tf_op jit(solution)/shard_map/ppermute | solution.py:291
  22.6 2.5 %collective-permute-start.5 = (bf16[256,1280]{1,0:T(8,128)(2,1)S(1)}, bf16[256,1280]{1,0:T(8,128)(2,1)S(1)}, u32[]{:S(2)}, u32[]{:S(2)}) collective-permute-start(bf16[256,1280]{1,0:T(8,128)(2,1)S(1)} %collective-permute-done.refs_0_), channel_id=1, source_target_pairs={{0,1},{1,0},{2,3},{3,2},{4,5},{5,4},{6,7},{7,6},{8,9},{9,8},{10,11... | collective-permute-start | bytes 1966088 | tf_op jit(solution)/shard_map/ppermute | solution.py:280
  22.6 3.0 %collective-permute-start.6 = (bf16[256,1280]{1,0:T(8,128)(2,1)S(1)}, bf16[256,1280]{1,0:T(8,128)(2,1)S(1)}, u32[]{:S(2)}, u32[]{:S(2)}) collective-permute-start(bf16[256,1280]{1,0:T(8,128)(2,1)S(1)} %collective-permute-done.1.refs_2_), channel_id=1, source_target_pairs={{0,1},{1,0},{2,3},{3,2},{4,5},{5,4},{6,7},{7,6},{8,9},{9,8},{10,11... | collective-permute-start | bytes 1966088 | tf_op jit(solution)/shard_map/ppermute | solution.py:280
  23.1 20.1 %collective-permute-start.3 = (bf16[256,1280]{1,0:T(8,128)(2,1)S(1)}, bf16[256,1280]{1,0:T(8,128)(2,1)S(1)}, u32[]{:S(2)}, u32[]{:S(2)}) collective-permute-start(bf16[256,1280]{1,0:T(8,128)(2,1)S(1)} %collective-permute-done.refs_0_), channel_id=1, source_target_pairs={{0,4},{4,8},{8,12},{12,14},{14,10},{10,6},{6,2},{2,0},{1,5},{5,9},... | collective-permute-start | bytes 1966088 | tf_op jit(solution)/shard_map/ppermute | solution.py:290
  24.7 18.6 %collective-permute-start.4 = (bf16[256,1280]{1,0:T(8,128)(2,1)S(1)}, bf16[256,1280]{1,0:T(8,128)(2,1)S(1)}, u32[]{:S(2)}, u32[]{:S(2)}) collective-permute-start(bf16[256,1280]{1,0:T(8,128)(2,1)S(1)} %collective-permute-done.1.refs_2_), channel_id=1, source_target_pairs={{4,0},{8,4},{12,8},{14,12},{10,14},{6,10},{2,6},{0,2},{5,1},{9,5},... | collective-permute-start | bytes 1966088 | tf_op jit(solution)/shard_map/ppermute | solution.py:291
  43.3 2.6 %collective-permute-start.10 = (bf16[256,1280]{1,0:T(8,128)(2,1)S(1)}, bf16[256,1280]{1,0:T(8,128)(2,1)S(1)}, u32[]{:S(2)}, u32[]{:S(2)}) collective-permute-start(bf16[256,1280]{1,0:T(8,128)(2,1)S(1)} %collective-permute-done.4.refs_2_), channel_id=1, source_target_pairs={{0,1},{1,0},{2,3},{3,2},{4,5},{5,4},{6,7},{7,6},{8,9},{9,8},{10,11... | collective-permute-start | bytes 1966088 | tf_op jit(solution)/shard_map/ppermute | solution.py:280
  43.4 2.9 %collective-permute-start.9 = (bf16[256,1280]{1,0:T(8,128)(2,1)S(1)}, bf16[256,1280]{1,0:T(8,128)(2,1)S(1)}, u32[]{:S(2)}, u32[]{:S(2)}) collective-permute-start(bf16[256,1280]{1,0:T(8,128)(2,1)S(1)} %collective-permute-done.3.refs_0_), channel_id=1, source_target_pairs={{0,1},{1,0},{2,3},{3,2},{4,5},{5,4},{6,7},{7,6},{8,9},{9,8},{10,11... | collective-permute-start | bytes 1966088 | tf_op jit(solution)/shard_map/ppermute | solution.py:280
  43.8 20.2 %collective-permute-start.7 = (bf16[256,1280]{1,0:T(8,128)(2,1)S(1)}, bf16[256,1280]{1,0:T(8,128)(2,1)S(1)}, u32[]{:S(2)}, u32[]{:S(2)}) collective-permute-start(bf16[256,1280]{1,0:T(8,128)(2,1)S(1)} %collective-permute-done.3.refs_0_), channel_id=1, source_target_pairs={{0,4},{4,8},{8,12},{12,14},{14,10},{10,6},{6,2},{2,0},{1,5},{5,9},... | collective-permute-start | bytes 1966088 | tf_op jit(solution)/shard_map/ppermute | solution.py:290
  45.5 18.6 %collective-permute-start.8 = (bf16[256,1280]{1,0:T(8,128)(2,1)S(1)}, bf16[256,1280]{1,0:T(8,128)(2,1)S(1)}, u32[]{:S(2)}, u32[]{:S(2)}) collective-permute-start(bf16[256,1280]{1,0:T(8,128)(2,1)S(1)} %collective-permute-done.4.refs_2_), channel_id=1, source_target_pairs={{4,0},{8,4},{12,8},{14,12},{10,14},{6,10},{2,6},{0,2},{5,1},{9,5},... | collective-permute-start | bytes 1966088 | tf_op jit(solution)/shard_map/ppermute | solution.py:291
  64.0 2.7 %collective-permute-start.13 = (bf16[256,1280]{1,0:T(8,128)(2,1)S(1)}, bf16[256,1280]{1,0:T(8,128)(2,1)S(1)}, u32[]{:S(2)}, u32[]{:S(2)}) collective-permute-start(bf16[256,1280]{1,0:T(8,128)(2,1)S(1)} %collective-permute-done.7.refs_0_), channel_id=1, source_target_pairs={{0,1},{1,0},{2,3},{3,2},{4,5},{5,4},{6,7},{7,6},{8,9},{9,8},{10,11... | collective-permute-start | bytes 1966088 | tf_op jit(solution)/shard_map/ppermute | solution.py:280
  64.2 2.9 %collective-permute-start.14 = (bf16[256,1280]{1,0:T(8,128)(2,1)S(1)}, bf16[256,1280]{1,0:T(8,128)(2,1)S(1)}, u32[]{:S(2)}, u32[]{:S(2)}) collective-permute-start(bf16[256,1280]{1,0:T(8,128)(2,1)S(1)} %collective-permute-done.8.refs_2_), channel_id=1, source_target_pairs={{0,1},{1,0},{2,3},{3,2},{4,5},{5,4},{6,7},{7,6},{8,9},{9,8},{10,11... | collective-permute-start | bytes 1966088 | tf_op jit(solution)/shard_map/ppermute | solution.py:280
  64.7 20.1 %collective-permute-start.11 = (bf16[128,1280]{1,0:T(8,128)(2,1)S(1)}, bf16[128,1280]{1,0:T(8,128)(2,1)S(1)}, u32[]{:S(2)}, u32[]{:S(2)}) collective-permute-start(bf16[128,1280]{1,0:T(8,128)(2,1)S(1)} %slice.15), channel_id=1, source_target_pairs={{0,4},{4,8},{8,12},{12,14},{14,10},{10,6},{6,2},{2,0},{1,5},{5,9},... | collective-permute-start | bytes 983048 | tf_op jit(solution)/shard_map/ppermute | solution.py:290
  66.3 18.4 %collective-permute-start.12 = (bf16[128,1280]{1,0:T(8,128)(2,1)S(1)}, bf16[128,1280]{1,0:T(8,128)(2,1)S(1)}, u32[]{:S(2)}, u32[]{:S(2)}) collective-permute-start(bf16[128,1280]{1,0:T(8,128)(2,1)S(1)} %slice.16), channel_id=1, source_target_pairs={{4,0},{8,4},{12,8},{14,12},{10,14},{6,10},{2,6},{0,2},{5,1},{9,5},... | collective-permute-start | bytes 983048 | tf_op jit(solution)/shard_map/ppermute | solution.py:291
  84.8 1.7 %collective-permute-start.15 = (bf16[128,1280]{1,0:T(8,128)(2,1)S(1)}, bf16[128,1280]{1,0:T(8,128)(2,1)S(1)}, u32[]{:S(2)}, u32[]{:S(2)}) collective-permute-start(bf16[128,1280]{1,0:T(8,128)(2,1)S(1)} %collective-permute-done.11.refs_0_), channel_id=1, source_target_pairs={{0,1},{1,0},{2,3},{3,2},{4,5},{5,4},{6,7},{7,6},{8,9},{9,8},{10,11... | collective-permute-start | bytes 983048 | tf_op jit(solution)/shard_map/ppermute | solution.py:280
  85.0 1.9 %collective-permute-start.16 = (bf16[128,1280]{1,0:T(8,128)(2,1)S(1)}, bf16[128,1280]{1,0:T(8,128)(2,1)S(1)}, u32[]{:S(2)}, u32[]{:S(2)}) collective-permute-start(bf16[128,1280]{1,0:T(8,128)(2,1)S(1)} %collective-permute-done.12.refs_1_), channel_id=1, source_target_pairs={{0,1},{1,0},{2,3},{3,2},{4,5},{5,4},{6,7},{7,6},{8,9},{9,8},{10,11... | collective-permute-start | bytes 983048 | tf_op jit(solution)/shard_map/ppermute | solution.py:280
  131.6 2.9 %collective-permute-start.17 = (bf16[8,256,256]{2,1,0:T(8,128)(2,1)S(1)}, bf16[8,256,256]{2,1,0:T(8,128)(2,1)}, u32[]{:S(2)}, u32[]{:S(2)}) collective-permute-start(bf16[8,256,256]{2,1,0:T(8,128)(2,1)S(1)} %get-tuple-element.63), channel_id=1, source_target_pairs={{0,1},{1,0},{2,3},{3,2},{4,5},{5,4},{6,7},{7,6},{8,9},{9,8},{10,11... | collective-permute-start | bytes 3145736 | tf_op jit(solution)/shard_map/ppermute | solution.py:280
  136.1 9.2 %collective-permute-start.18 = (bf16[2,256,256]{2,1,0:T(8,128)(2,1)S(1)}, bf16[2,256,256]{2,1,0:T(8,128)(2,1)S(1)}, u32[]{:S(2)}, u32[]{:S(2)}) collective-permute-start(bf16[2,256,256]{2,1,0:T(8,128)(2,1)S(1)} %pad_maximum_fusion), channel_id=1, source_target_pairs={{0,2},{2,0},{4,6},{6,4},{8,10},{10,8},{12,14},{14,12},{1,3},{3,1},... | collective-permute-start | bytes 786440 | tf_op jit(solution)/shard_map/ppermute | solution.py:321
  136.3 13.7 %collective-permute-start.19 = (bf16[256,256]{1,0:T(8,128)(2,1)S(1)}, bf16[256,256]{1,0:T(8,128)(2,1)S(1)}, u32[]{:S(2)}, u32[]{:S(2)}) collective-permute-start(bf16[256,256]{1,0:T(8,128)(2,1)S(1)} %get-tuple-element.64), channel_id=1, source_target_pairs={{0,4},{2,6},{4,8},{6,10},{8,12},{10,14},{12,0},{14,2},{1,5},{3,7},... | collective-permute-start | bytes 393224 | tf_op jit(solution)/shard_map/ppermute | solution.py:321
  137.3 12.7 %collective-permute-start.20 = (bf16[256,256]{1,0:T(8,128)(2,1)S(1)}, bf16[256,256]{1,0:T(8,128)(2,1)S(1)}, u32[]{:S(2)}, u32[]{:S(2)}) collective-permute-start(bf16[256,256]{1,0:T(8,128)(2,1)S(1)} %get-tuple-element.67), channel_id=1, source_target_pairs={{0,6},{2,4},{4,10},{6,8},{8,14},{10,12},{12,2},{14,0},{1,7},{3,5},... | collective-permute-start | bytes 393224 | tf_op jit(solution)/shard_map/ppermute | solution.py:321
  139.2 10.8 %collective-permute-start.21 = (bf16[256,256]{1,0:T(8,128)(2,1)S(1)}, bf16[256,256]{1,0:T(8,128)(2,1)S(1)}, u32[]{:S(2)}, u32[]{:S(2)}) collective-permute-start(bf16[256,256]{1,0:T(8,128)(2,1)S(1)} %get-tuple-element.66), channel_id=1, source_target_pairs={{0,12},{2,14},{4,0},{6,2},{8,4},{10,6},{12,8},{14,10},{1,13},{3,15... | collective-permute-start | bytes 393224 | tf_op jit(solution)/shard_map/ppermute | solution.py:321
  141.8 10.4 %collective-permute-start.22 = (bf16[256,256]{1,0:T(8,128)(2,1)S(1)}, bf16[256,256]{1,0:T(8,128)(2,1)S(1)}, u32[]{:S(2)}, u32[]{:S(2)}) collective-permute-start(bf16[256,256]{1,0:T(8,128)(2,1)S(1)} %get-tuple-element.65), channel_id=1, source_target_pairs={{0,14},{2,12},{4,2},{6,0},{8,6},{10,4},{12,10},{14,8},{1,15},{3,13... | collective-permute-start | bytes 393224 | tf_op jit(solution)/shard_map/ppermute | solution.py:321
  146.3 11.4 %collective-permute-start.23 = (bf16[256,256]{1,0:T(8,128)(2,1)S(1)}, bf16[256,256]{1,0:T(8,128)(2,1)S(1)}, u32[]{:S(2)}, u32[]{:S(2)}) collective-permute-start(bf16[256,256]{1,0:T(8,128)(2,1)S(1)} %fusion.9), channel_id=1, source_target_pairs={{0,8},{2,10},{4,12},{6,14},{8,0},{10,2},{12,4},{14,6},{1,9},{3,11}... | collective-permute-start | bytes 393224 | tf_op jit(solution)/shard_map/ppermute | solution.py:321
  (1 other events, 33.0 us)

commit v5 on v4

--- a/solution.py
+++ b/solution.py
@@ -279,7 +279,13 @@
     def sibling(array):
         return lax.ppermute(array, "tok", SWAP)
 
-    mine = jnp.concatenate([teacher_hidden, student_hidden], axis=1)
+    wide = ((0, 0, 0), (0, ds, 0)), ((0, 0, 0), (dt, 0, 0))
+    nothing = jnp.zeros((), teacher_hidden.dtype)
+    mine = jnp.where(
+        lax.broadcasted_iota(jnp.int32, (teacher_hidden.shape[0], dt + ds), 1) < dt,
+        lax.pad(teacher_hidden, nothing, wide[0]),
+        lax.pad(student_hidden, nothing, wide[1]),
+    )
     half = mine.shape[0] // 2
     wt, ws = teacher_weight.T, student_weight.T
     from_low = from_high = mine

time: 160 us -> 159 us (level)
  local copies, waits for them, and re-layouts: 3.36 us -> 1.37 us
where the time goes in v5:
time: 159 us
  Pallas kernels  93 us (58%)
  starting transfers between devices  21.7 us (14%)
  waiting for transfers between devices  21.2 us (13%)
  blocking collectives  14.8 us (9%)
  other arithmetic  5.5 us (3%)
    pallas_call x5, Pallas kernels, stage(): pl.pallas_call(functools.partial(stage_kernel, count, pieces, dt, held is...  77.8 us
    pallas_call x1, Pallas kernels, grad_partial(): pl.pallas_call(functools.partial(grad_kernel, block), grid_spec=pltpu.Pre...  15.2 us
    all_to_all x1, blocking collectives, ringed(): every = lax.all_to_all(stats, ('vocab', 'tok'), 0, 0, tiled=True)  14.8 us
    ppermute x6, starting transfers between devices, sent(): lax.ppermute(value, 'vocab', [(c, goal(c, shift, flip)) for c in range(co...  10.1 us
    ppermute x6, waiting for transfers between devices, sent(): lax.ppermute(value, 'vocab', [(c, goal(c, shift, flip)) for c in range(co...  9.86 us
    ppermute x4, starting transfers between devices, ringed(): next_low = lax.ppermute(from_low[:half] if final else from_low, 'vocab', up)  7.47 us
    ppermute x10, waiting for transfers between devices, sibling(): return lax.ppermute(array, 'tok', SWAP)  5.61 us
    ppermute x4, waiting for transfers between devices, ringed(): next_low = lax.ppermute(from_low[:half] if final else from_low, 'vocab', up)  4.25 us
  transfers between devices with their start and end apart: 24, of which 11 were waited for; matrix products, arithmetic and copies ran while one was open for 1% of the time, Pallas kernels for 40%

profile of v5, /device:TPU:0, one launch (start us, length us, event | category | flops | bytes accessed | tf_op | source)
XLA Modules:
  0.0 158.6 jit_solution(12441219876368937959)
XLA Ops:
  0.6 1.2 pad_select_fusion.refs_0_
  2.4 2.6 %collective-permute-start = (bf16[256,1280]{1,0:T(8,128)(2,1)S(1)}, bf16[256,1280]{1,0:T(8,128)(2,1)S(1)}, u32[]{:S(2)}, u32[]{:S(2)}) collective-permute-start(bf16[256,1280]{1,0:T(8,128)(2,1)S(1)} %pad_select_fusion.refs_0_), channel_id=1, source_target_pairs={{0,4},{4,8},{8,12},{12,14},{14,10},{10,6},{6,2},{2,0},{1,5},{5,9},... | collective-permute-start | bytes 1966088 | tf_op jit(solution)/shard_map/ppermute | solution.py:296
  5.8 10.2 %stage.4 = (f32[4752,512]{1,0:T(8,128)S(1)}, f32[4752,512]{1,0:T(8,128)S(1)}) custom-call(s32[9]{0:T(128)S(1)} %pad_add_fusion.off_ref, bf16[256,1280]{1,0:T(8,128)(2,1)S(1)} %pad_select_fusion.refs_0_, bf16[256,1280]{1,0:T(8,128)(2,1)S(1)} %collective-permute-done.2.refs_1_, bf16[4752,8192]{1,0:T(8,128)(2,1)} %bitcast.2.refs_2_.refs_4_.refs_5_, ...), custom_call_target="tpu_custom_call" | custom-call | flops 6228541440 | bytes 12165120 | tf_op jit(solution)/shard_map/stage/pallas_call | solution.py:163
  16.1 4.2 %collective-permute-done.refs_0_ = bf16[256,1280]{1,0:T(8,128)(2,1)S(1)} collective-permute-done((bf16[256,1280]{1,0:T(8,128)(2,1)S(1)}, bf16[256,1280]{1,0:T(8,128)(2,1)S(1)}, u32[]{:S(2)}, u32[]{:S(2)}) %collective-permute-start) | collective-permute-done | bytes 655392 | tf_op jit(solution)/shard_map/ppermute | solution.py:296
  20.3 1.5 collective-permute-done.1.refs_2_
  22.4 1.6 collective-permute-start.3
  24.9 17.6 %stage.5 = (f32[4752,512]{1,0:T(8,128)S(1)}, f32[4752,512]{1,0:T(8,128)S(1)}) custom-call(s32[9]{0:T(128)S(1)} %pad_add_fusion.off_ref, bf16[256,1280]{1,0:T(8,128)(2,1)S(1)} %collective-permute-done.refs_0_, bf16[256,1280]{1,0:T(8,128)(2,1)S(1)} %collective-permute-done.5.refs_1_, ...), custom_call_target="tpu_custom_call", output_to_operand_aliasing={{0}: (9, {}), {1}: (10, {})} | custom-call | flops 12457082880 | bytes 24330240 | tf_op jit(solution)/shard_map/stage/pallas_call | solution.py:163
  43.1 1.6 %collective-permute-start.7 = (bf16[256,1280]{1,0:T(8,128)(2,1)S(1)}, bf16[256,1280]{1,0:T(8,128)(2,1)S(1)}, u32[]{:S(2)}, u32[]{:S(2)}) collective-permute-start(bf16[256,1280]{1,0:T(8,128)(2,1)S(1)} %collective-permute-done.3.refs_0_), channel_id=1, source_target_pairs={{0,4},{4,8},{8,12},{12,14},{14,10},{10,6},{6,2},{2,0},{1,5},{5,9},... | collective-permute-start | bytes 1966088 | tf_op jit(solution)/shard_map/ppermute | solution.py:296
  45.6 17.7 %stage.6 = (f32[4752,512]{1,0:T(8,128)S(1)}, f32[4752,512]{1,0:T(8,128)S(1)}) custom-call(s32[9]{0:T(128)S(1)} %pad_add_fusion.off_ref, bf16[256,1280]{1,0:T(8,128)(2,1)S(1)} %collective-permute-done.3.refs_0_, bf16[256,1280]{1,0:T(8,128)(2,1)S(1)} %collective-permute-done.9.refs_1_, ...), custom_call_target="tpu_custom_call", output_to_operand_aliasing={{0}: (9, {}), {1}: (10, {})} | custom-call | flops 12457082880 | bytes 24330240 | tf_op jit(solution)/shard_map/stage/pallas_call | solution.py:163
  63.9 1.7 %collective-permute-start.11 = (bf16[128,1280]{1,0:T(8,128)(2,1)S(1)}, bf16[128,1280]{1,0:T(8,128)(2,1)S(1)}, u32[]{:S(2)}, u32[]{:S(2)}) collective-permute-start(bf16[128,1280]{1,0:T(8,128)(2,1)S(1)} %slice.15), channel_id=1, source_target_pairs={{0,4},{4,8},{8,12},{12,14},{14,10},{10,6},{6,2},{2,0},{1,5},{5,9},... | collective-permute-start | bytes 983048 | tf_op jit(solution)/shard_map/ppermute | solution.py:296
  66.4 17.6 %stage.7 = (f32[4752,512]{1,0:T(8,128)S(1)}, f32[4752,512]{1,0:T(8,128)S(1)}) custom-call(s32[9]{0:T(128)S(1)} %pad_add_fusion.off_ref, bf16[256,1280]{1,0:T(8,128)(2,1)S(1)} %collective-permute-done.7.refs_0_, bf16[256,1280]{1,0:T(8,128)(2,1)S(1)} %collective-permute-done.13.refs_1_, ...), custom_call_target="tpu_custom_call", output_to_operand_aliasing={{0}: (9, {}), {1}: (10, {})} | custom-call | flops 12457082880 | bytes 24330240 | tf_op jit(solution)/shard_map/stage/pallas_call | solution.py:163
  86.2 14.7 %stage_last.1 = (f32[4752,512]{1,0:T(8,128)S(1)}, f32[4752,512]{1,0:T(8,128)S(1)}, f32[5,8,512]{2,1,0:T(8,128)S(1)}, f32[16,8,512]{2,1,0:T(8,128)S(1)}) custom-call(s32[9]{0:T(128)S(1)} %pad_add_fusion.off_ref, bf16[128,1280]{1,0:T(8,128)(2,1)S(1)} %collective-permute-done.11.refs_0_, ...), custom_call_target="tpu_custom_call", output_to_operand_aliasing={{0}: (7, {}), {1}: (8, {})} | custom-call | flops 6228541440 | bytes 12165120 | tf_op jit(solution)/shard_map/stage_last/pallas_call | solution.py:163
  100.9 14.8 %all_to_all.5.stats = f32[16,8,512]{2,1,0:T(8,128)S(1)} all-to-all(f32[16,8,512]{2,1,0:T(8,128)S(1)} %get-tuple-element.57), channel_id=1, replica_groups=mesh['groups'=2,'vocab'=8,'tok'=2] {'vocab','tok'}, dimensions={0} | all-to-all | bytes 524288 | tf_op jit(solution)/shard_map/all_to_all | solution.py:307
  115.7 15.2 %grad.1 = (f32[1,512]{1,0:T(1,128)S(1)}, f32[8,256,256]{2,1,0:T(8,128)S(1)}, bf16[8,256,256]{2,1,0:T(8,128)(2,1)S(1)}) custom-call(s32[9]{0:T(128)S(1)} %pad_add_fusion.off_ref, f32[16,8,512]{2,1,0:T(8,128)S(1)} %all_to_all.5.stats, f32[5,8,512]{2,1,0:T(8,128)S(1)} %get-tuple-element.58.tops, f32[4752,512]{1,0:T(8,128)S(1)} %get-tuple-element.59.t_exp, ...), custom_call_target="tpu_custom_call" | custom-call | flops 9965666304 | bytes 19464192 | tf_op jit(solution)/shard_map/grad/pallas_call | solution.py:232
  131.1 2.6 %collective-permute-done.17 = bf16[8,256,256]{2,1,0:T(8,128)(2,1)} collective-permute-done((bf16[8,256,256]{2,1,0:T(8,128)(2,1)S(1)}, bf16[8,256,256]{2,1,0:T(8,128)(2,1)}, u32[]{:S(2)}, u32[]{:S(2)}) %collective-permute-start.17) | collective-permute-done | bytes 1048608 | tf_op jit(solution)/shard_map/ppermute | solution.py:280
  133.8 1.5 add_convert_fusion
  136.6 1.9 %collective-permute-start.20 = (bf16[256,256]{1,0:T(8,128)(2,1)S(1)}, bf16[256,256]{1,0:T(8,128)(2,1)S(1)}, u32[]{:S(2)}, u32[]{:S(2)}) collective-permute-start(bf16[256,256]{1,0:T(8,128)(2,1)S(1)} %get-tuple-element.67), channel_id=1, source_target_pairs={{0,6},{2,4},{4,10},{6,8},{8,14},{10,12},{12,2},{14,0},{1,7},{3,5},... | collective-permute-start | bytes 393224 | tf_op jit(solution)/shard_map/ppermute | solution.py:327
  138.5 2.5 %collective-permute-start.21 = (bf16[256,256]{1,0:T(8,128)(2,1)S(1)}, bf16[256,256]{1,0:T(8,128)(2,1)S(1)}, u32[]{:S(2)}, u32[]{:S(2)}) collective-permute-start(bf16[256,256]{1,0:T(8,128)(2,1)S(1)} %get-tuple-element.66), channel_id=1, source_target_pairs={{0,12},{2,14},{4,0},{6,2},{8,4},{10,6},{12,8},{14,10},{1,13},{3,15... | collective-permute-start | bytes 393224 | tf_op jit(solution)/shard_map/ppermute | solution.py:327
  141.0 1.3 collective-permute-start.22
  142.3 2.2 %collective-permute-done.18 = bf16[2,256,256]{2,1,0:T(8,128)(2,1)S(1)} collective-permute-done((bf16[2,256,256]{2,1,0:T(8,128)(2,1)S(1)}, bf16[2,256,256]{2,1,0:T(8,128)(2,1)S(1)}, u32[]{:S(2)}, u32[]{:S(2)}) %collective-permute-start.18) | collective-permute-done | bytes 262176 | tf_op jit(solution)/shard_map/ppermute | solution.py:327
  145.6 3.1 %collective-permute-start.23 = (bf16[256,256]{1,0:T(8,128)(2,1)S(1)}, bf16[256,256]{1,0:T(8,128)(2,1)S(1)}, u32[]{:S(2)}, u32[]{:S(2)}) collective-permute-start(bf16[256,256]{1,0:T(8,128)(2,1)S(1)} %fusion.9), channel_id=1, source_target_pairs={{0,8},{2,10},{4,12},{6,14},{8,0},{10,2},{12,4},{14,6},{1,9},{3,11}... | collective-permute-start | bytes 393224 | tf_op jit(solution)/shard_map/ppermute | solution.py:327
  149.3 2.2 %collective-permute-done.22 = bf16[256,256]{1,0:T(8,128)(2,1)S(1)} collective-permute-done((bf16[256,256]{1,0:T(8,128)(2,1)S(1)}, bf16[256,256]{1,0:T(8,128)(2,1)S(1)}, u32[]{:S(2)}, u32[]{:S(2)}) %collective-permute-start.22) | collective-permute-done | bytes 131104 | tf_op jit(solution)/shard_map/ppermute | solution.py:327
  151.4 5.5 %collective-permute-done.23 = bf16[256,256]{1,0:T(8,128)(2,1)S(1)} collective-permute-done((bf16[256,256]{1,0:T(8,128)(2,1)S(1)}, bf16[256,256]{1,0:T(8,128)(2,1)S(1)}, u32[]{:S(2)}, u32[]{:S(2)}) %collective-permute-start.23) | collective-permute-done | bytes 131104 | tf_op jit(solution)/shard_map/ppermute | solution.py:327
  156.9 1.7 %fusion.8 = bf16[256,256]{1,0:T(8,128)(2,1)} fusion(f32[2,256,256]{2,1,0:T(8,128)S(1)} %convert_element_type.48, bf16[256,256]{1,0:T(8,128)(2,1)S(1)} %collective-permute-done.23, bf16[256,256]{1,0:T(8,128)(2,1)S(1)} %collective-permute-done.22, bf16[256,256]{1,0:T(8,128)(2,1)S(1)} %collective-permute-done.21, ...), kind=kLoop, calls=%fused_computation.12 | loop fusion | flops 983040 | bytes 1442820 | tf_op jit(solution)/shard_map/convert_element_type | solution.py:338
  (47 shorter events, 10.8 us)
Async XLA Ops:
  1.9 4.0 %collective-permute-start.2 = (bf16[256,1280]{1,0:T(8,128)(2,1)S(1)}, bf16[256,1280]{1,0:T(8,128)(2,1)S(1)}, u32[]{:S(2)}, u32[]{:S(2)}) collective-permute-start(bf16[256,1280]{1,0:T(8,128)(2,1)S(1)} %pad_select_fusion.refs_0_), channel_id=1, source_target_pairs={{0,1},{1,0},{2,3},{3,2},{4,5},{5,4},{6,7},{7,6},{8,9},{9,8},{10,11... | collective-permute-start | bytes 1966088 | tf_op jit(solution)/shard_map/ppermute | solution.py:280
  2.4 17.9 %collective-permute-start = (bf16[256,1280]{1,0:T(8,128)(2,1)S(1)}, bf16[256,1280]{1,0:T(8,128)(2,1)S(1)}, u32[]{:S(2)}, u32[]{:S(2)}) collective-permute-start(bf16[256,1280]{1,0:T(8,128)(2,1)S(1)} %pad_select_fusion.refs_0_), channel_id=1, source_target_pairs={{0,4},{4,8},{8,12},{12,14},{14,10},{10,6},{6,2},{2,0},{1,5},{5,9},... | collective-permute-start | bytes 1966088 | tf_op jit(solution)/shard_map/ppermute | solution.py:296
  5.0 16.8 %collective-permute-start.1 = (bf16[256,1280]{1,0:T(8,128)(2,1)S(1)}, bf16[256,1280]{1,0:T(8,128)(2,1)S(1)}, u32[]{:S(2)}, u32[]{:S(2)}) collective-permute-start(bf16[256,1280]{1,0:T(8,128)(2,1)S(1)} %pad_select_fusion.refs_0_), channel_id=1, source_target_pairs={{4,0},{8,4},{12,8},{14,12},{10,14},{6,10},{2,6},{0,2},{5,1},{9,5},... | collective-permute-start | bytes 1966088 | tf_op jit(solution)/shard_map/ppermute | solution.py:297
  21.8 2.5 %collective-permute-start.5 = (bf16[256,1280]{1,0:T(8,128)(2,1)S(1)}, bf16[256,1280]{1,0:T(8,128)(2,1)S(1)}, u32[]{:S(2)}, u32[]{:S(2)}) collective-permute-start(bf16[256,1280]{1,0:T(8,128)(2,1)S(1)} %collective-permute-done.refs_0_), channel_id=1, source_target_pairs={{0,1},{1,0},{2,3},{3,2},{4,5},{5,4},{6,7},{7,6},{8,9},{9,8},{10,11... | collective-permute-start | bytes 1966088 | tf_op jit(solution)/shard_map/ppermute | solution.py:280
  21.8 3.0 %collective-permute-start.6 = (bf16[256,1280]{1,0:T(8,128)(2,1)S(1)}, bf16[256,1280]{1,0:T(8,128)(2,1)S(1)}, u32[]{:S(2)}, u32[]{:S(2)}) collective-permute-start(bf16[256,1280]{1,0:T(8,128)(2,1)S(1)} %collective-permute-done.1.refs_2_), channel_id=1, source_target_pairs={{0,1},{1,0},{2,3},{3,2},{4,5},{5,4},{6,7},{7,6},{8,9},{9,8},{10,11... | collective-permute-start | bytes 1966088 | tf_op jit(solution)/shard_map/ppermute | solution.py:280
  22.4 20.1 %collective-permute-start.3 = (bf16[256,1280]{1,0:T(8,128)(2,1)S(1)}, bf16[256,1280]{1,0:T(8,128)(2,1)S(1)}, u32[]{:S(2)}, u32[]{:S(2)}) collective-permute-start(bf16[256,1280]{1,0:T(8,128)(2,1)S(1)} %collective-permute-done.refs_0_), channel_id=1, source_target_pairs={{0,4},{4,8},{8,12},{12,14},{14,10},{10,6},{6,2},{2,0},{1,5},{5,9},... | collective-permute-start | bytes 1966088 | tf_op jit(solution)/shard_map/ppermute | solution.py:296
  23.9 18.6 %collective-permute-start.4 = (bf16[256,1280]{1,0:T(8,128)(2,1)S(1)}, bf16[256,1280]{1,0:T(8,128)(2,1)S(1)}, u32[]{:S(2)}, u32[]{:S(2)}) collective-permute-start(bf16[256,1280]{1,0:T(8,128)(2,1)S(1)} %collective-permute-done.1.refs_2_), channel_id=1, source_target_pairs={{4,0},{8,4},{12,8},{14,12},{10,14},{6,10},{2,6},{0,2},{5,1},{9,5},... | collective-permute-start | bytes 1966088 | tf_op jit(solution)/shard_map/ppermute | solution.py:297
  42.5 2.6 %collective-permute-start.10 = (bf16[256,1280]{1,0:T(8,128)(2,1)S(1)}, bf16[256,1280]{1,0:T(8,128)(2,1)S(1)}, u32[]{:S(2)}, u32[]{:S(2)}) collective-permute-start(bf16[256,1280]{1,0:T(8,128)(2,1)S(1)} %collective-permute-done.4.refs_2_), channel_id=1, source_target_pairs={{0,1},{1,0},{2,3},{3,2},{4,5},{5,4},{6,7},{7,6},{8,9},{9,8},{10,11... | collective-permute-start | bytes 1966088 | tf_op jit(solution)/shard_map/ppermute | solution.py:280
  42.7 2.9 %collective-permute-start.9 = (bf16[256,1280]{1,0:T(8,128)(2,1)S(1)}, bf16[256,1280]{1,0:T(8,128)(2,1)S(1)}, u32[]{:S(2)}, u32[]{:S(2)}) collective-permute-start(bf16[256,1280]{1,0:T(8,128)(2,1)S(1)} %collective-permute-done.3.refs_0_), channel_id=1, source_target_pairs={{0,1},{1,0},{2,3},{3,2},{4,5},{5,4},{6,7},{7,6},{8,9},{9,8},{10,11... | collective-permute-start | bytes 1966088 | tf_op jit(solution)/shard_map/ppermute | solution.py:280
  43.1 20.2 %collective-permute-start.7 = (bf16[256,1280]{1,0:T(8,128)(2,1)S(1)}, bf16[256,1280]{1,0:T(8,128)(2,1)S(1)}, u32[]{:S(2)}, u32[]{:S(2)}) collective-permute-start(bf16[256,1280]{1,0:T(8,128)(2,1)S(1)} %collective-permute-done.3.refs_0_), channel_id=1, source_target_pairs={{0,4},{4,8},{8,12},{12,14},{14,10},{10,6},{6,2},{2,0},{1,5},{5,9},... | collective-permute-start | bytes 1966088 | tf_op jit(solution)/shard_map/ppermute | solution.py:296
  44.7 18.6 %collective-permute-start.8 = (bf16[256,1280]{1,0:T(8,128)(2,1)S(1)}, bf16[256,1280]{1,0:T(8,128)(2,1)S(1)}, u32[]{:S(2)}, u32[]{:S(2)}) collective-permute-start(bf16[256,1280]{1,0:T(8,128)(2,1)S(1)} %collective-permute-done.4.refs_2_), channel_id=1, source_target_pairs={{4,0},{8,4},{12,8},{14,12},{10,14},{6,10},{2,6},{0,2},{5,1},{9,5},... | collective-permute-start | bytes 1966088 | tf_op jit(solution)/shard_map/ppermute | solution.py:297
  63.3 2.7 %collective-permute-start.13 = (bf16[256,1280]{1,0:T(8,128)(2,1)S(1)}, bf16[256,1280]{1,0:T(8,128)(2,1)S(1)}, u32[]{:S(2)}, u32[]{:S(2)}) collective-permute-start(bf16[256,1280]{1,0:T(8,128)(2,1)S(1)} %collective-permute-done.7.refs_0_), channel_id=1, source_target_pairs={{0,1},{1,0},{2,3},{3,2},{4,5},{5,4},{6,7},{7,6},{8,9},{9,8},{10,11... | collective-permute-start | bytes 1966088 | tf_op jit(solution)/shard_map/ppermute | solution.py:280
  63.5 2.9 %collective-permute-start.14 = (bf16[256,1280]{1,0:T(8,128)(2,1)S(1)}, bf16[256,1280]{1,0:T(8,128)(2,1)S(1)}, u32[]{:S(2)}, u32[]{:S(2)}) collective-permute-start(bf16[256,1280]{1,0:T(8,128)(2,1)S(1)} %collective-permute-done.8.refs_2_), channel_id=1, source_target_pairs={{0,1},{1,0},{2,3},{3,2},{4,5},{5,4},{6,7},{7,6},{8,9},{9,8},{10,11... | collective-permute-start | bytes 1966088 | tf_op jit(solution)/shard_map/ppermute | solution.py:280
  63.9 20.1 %collective-permute-start.11 = (bf16[128,1280]{1,0:T(8,128)(2,1)S(1)}, bf16[128,1280]{1,0:T(8,128)(2,1)S(1)}, u32[]{:S(2)}, u32[]{:S(2)}) collective-permute-start(bf16[128,1280]{1,0:T(8,128)(2,1)S(1)} %slice.15), channel_id=1, source_target_pairs={{0,4},{4,8},{8,12},{12,14},{14,10},{10,6},{6,2},{2,0},{1,5},{5,9},... | collective-permute-start | bytes 983048 | tf_op jit(solution)/shard_map/ppermute | solution.py:296
  65.6 18.4 %collective-permute-start.12 = (bf16[128,1280]{1,0:T(8,128)(2,1)S(1)}, bf16[128,1280]{1,0:T(8,128)(2,1)S(1)}, u32[]{:S(2)}, u32[]{:S(2)}) collective-permute-start(bf16[128,1280]{1,0:T(8,128)(2,1)S(1)} %slice.16), channel_id=1, source_target_pairs={{4,0},{8,4},{12,8},{14,12},{10,14},{6,10},{2,6},{0,2},{5,1},{9,5},... | collective-permute-start | bytes 983048 | tf_op jit(solution)/shard_map/ppermute | solution.py:297
  84.0 1.7 %collective-permute-start.15 = (bf16[128,1280]{1,0:T(8,128)(2,1)S(1)}, bf16[128,1280]{1,0:T(8,128)(2,1)S(1)}, u32[]{:S(2)}, u32[]{:S(2)}) collective-permute-start(bf16[128,1280]{1,0:T(8,128)(2,1)S(1)} %collective-permute-done.11.refs_0_), channel_id=1, source_target_pairs={{0,1},{1,0},{2,3},{3,2},{4,5},{5,4},{6,7},{7,6},{8,9},{9,8},{10,11... | collective-permute-start | bytes 983048 | tf_op jit(solution)/shard_map/ppermute | solution.py:280
  84.2 1.9 %collective-permute-start.16 = (bf16[128,1280]{1,0:T(8,128)(2,1)S(1)}, bf16[128,1280]{1,0:T(8,128)(2,1)S(1)}, u32[]{:S(2)}, u32[]{:S(2)}) collective-permute-start(bf16[128,1280]{1,0:T(8,128)(2,1)S(1)} %collective-permute-done.12.refs_1_), channel_id=1, source_target_pairs={{0,1},{1,0},{2,3},{3,2},{4,5},{5,4},{6,7},{7,6},{8,9},{9,8},{10,11... | collective-permute-start | bytes 983048 | tf_op jit(solution)/shard_map/ppermute | solution.py:280
  130.9 2.9 %collective-permute-start.17 = (bf16[8,256,256]{2,1,0:T(8,128)(2,1)S(1)}, bf16[8,256,256]{2,1,0:T(8,128)(2,1)}, u32[]{:S(2)}, u32[]{:S(2)}) collective-permute-start(bf16[8,256,256]{2,1,0:T(8,128)(2,1)S(1)} %get-tuple-element.63), channel_id=1, source_target_pairs={{0,1},{1,0},{2,3},{3,2},{4,5},{5,4},{6,7},{7,6},{8,9},{9,8},{10,11... | collective-permute-start | bytes 3145736 | tf_op jit(solution)/shard_map/ppermute | solution.py:280
  135.3 9.2 %collective-permute-start.18 = (bf16[2,256,256]{2,1,0:T(8,128)(2,1)S(1)}, bf16[2,256,256]{2,1,0:T(8,128)(2,1)S(1)}, u32[]{:S(2)}, u32[]{:S(2)}) collective-permute-start(bf16[2,256,256]{2,1,0:T(8,128)(2,1)S(1)} %pad_maximum_fusion), channel_id=1, source_target_pairs={{0,2},{2,0},{4,6},{6,4},{8,10},{10,8},{12,14},{14,12},{1,3},{3,1},... | collective-permute-start | bytes 786440 | tf_op jit(solution)/shard_map/ppermute | solution.py:327
  135.6 13.7 %collective-permute-start.19 = (bf16[256,256]{1,0:T(8,128)(2,1)S(1)}, bf16[256,256]{1,0:T(8,128)(2,1)S(1)}, u32[]{:S(2)}, u32[]{:S(2)}) collective-permute-start(bf16[256,256]{1,0:T(8,128)(2,1)S(1)} %get-tuple-element.64), channel_id=1, source_target_pairs={{0,4},{2,6},{4,8},{6,10},{8,12},{10,14},{12,0},{14,2},{1,5},{3,7},... | collective-permute-start | bytes 393224 | tf_op jit(solution)/shard_map/ppermute | solution.py:327
  136.6 12.7 %collective-permute-start.20 = (bf16[256,256]{1,0:T(8,128)(2,1)S(1)}, bf16[256,256]{1,0:T(8,128)(2,1)S(1)}, u32[]{:S(2)}, u32[]{:S(2)}) collective-permute-start(bf16[256,256]{1,0:T(8,128)(2,1)S(1)} %get-tuple-element.67), channel_id=1, source_target_pairs={{0,6},{2,4},{4,10},{6,8},{8,14},{10,12},{12,2},{14,0},{1,7},{3,5},... | collective-permute-start | bytes 393224 | tf_op jit(solution)/shard_map/ppermute | solution.py:327
  138.5 10.8 %collective-permute-start.21 = (bf16[256,256]{1,0:T(8,128)(2,1)S(1)}, bf16[256,256]{1,0:T(8,128)(2,1)S(1)}, u32[]{:S(2)}, u32[]{:S(2)}) collective-permute-start(bf16[256,256]{1,0:T(8,128)(2,1)S(1)} %get-tuple-element.66), channel_id=1, source_target_pairs={{0,12},{2,14},{4,0},{6,2},{8,4},{10,6},{12,8},{14,10},{1,13},{3,15... | collective-permute-start | bytes 393224 | tf_op jit(solution)/shard_map/ppermute | solution.py:327
  141.0 10.4 %collective-permute-start.22 = (bf16[256,256]{1,0:T(8,128)(2,1)S(1)}, bf16[256,256]{1,0:T(8,128)(2,1)S(1)}, u32[]{:S(2)}, u32[]{:S(2)}) collective-permute-start(bf16[256,256]{1,0:T(8,128)(2,1)S(1)} %get-tuple-element.65), channel_id=1, source_target_pairs={{0,14},{2,12},{4,2},{6,0},{8,6},{10,4},{12,10},{14,8},{1,15},{3,13... | collective-permute-start | bytes 393224 | tf_op jit(solution)/shard_map/ppermute | solution.py:327
  145.6 11.4 %collective-permute-start.23 = (bf16[256,256]{1,0:T(8,128)(2,1)S(1)}, bf16[256,256]{1,0:T(8,128)(2,1)S(1)}, u32[]{:S(2)}, u32[]{:S(2)}) collective-permute-start(bf16[256,256]{1,0:T(8,128)(2,1)S(1)} %fusion.9), channel_id=1, source_target_pairs={{0,8},{2,10},{4,12},{6,14},{8,0},{10,2},{12,4},{14,6},{1,9},{3,11}... | collective-permute-start | bytes 393224 | tf_op jit(solution)/shard_map/ppermute | solution.py:327
  (1 other events, 33.0 us)
